TPU v7x, 256 devices: a whole 4x4x8 slice. The times are simulated.
256 devices in a mesh: node: 64 (over y, z, core), feat: 4 (over x).
Axes of the slice: x: 4, y: 4, z: 8, core: 2. Of those that a mesh axis runs over, the one named last changes fastest.
Arguments:
- features: bfloat16 [32768, 128], P('node', 'feat'), may hold values from -10 to 10
- send_rows: int32 [64, 64, 64], P('node'), may hold values from 0 to 511
- send_count: int32 [64, 64], P('node'), may hold values from 1 to 64, 2048 in all within a row
- tile_src: int32 [256, 16], P('node'), may hold values from 0 to 35
- tile_val: bfloat16 [256, 16, 128, 128], P('node'), may hold values from 0 to 0.0009765625
- labels: int32 [32768], P('node'), may hold values from 0 to 171
- w_self1: bfloat16 [128, 1024], P('feat'), may hold values from -0.5 to 0.5
- w_neigh1: bfloat16 [128, 1024], P('feat'), may hold values from -0.5 to 0.5
- w_self2: bfloat16 [1024, 172], P('feat'), may hold values from -0.5 to 0.5
- w_neigh2: bfloat16 [1024, 172], P('feat'), may hold values from -0.1875 to 0.1875
Outputs:
- mean_loss: float32 [], replicated
- grad_self1: float32 [128, 1024], P('feat')
- grad_neigh1: float32 [128, 1024], P('feat')
- grad_self2: float32 [1024, 172], P('feat')
- grad_neigh2: float32 [1024, 172], P('feat')
Inputs may be any that keep to these rules, and one draw needn't show every extreme that they name: `send_rows`: row indices within the sending partition's 512 rows. Each row of send_count sums to 2048 and holds 64 at least once. `tile_src`: block numbers of the destination partition's source rows: numbers below 4 name its own rows, the others its halo slots.
All inputs are finite; a program needn't handle non-finite values.
Results may differ from a plain program's by a relative error of at most 0.00095.
The roundings to bfloat16 on the way count: a program that leaves them out, or rounds other values in their place, can miss the bound.
Values may be sent and summed in bfloat16 or wider, within the bound.
A program may use at most 64 MiB of HBM per device.

v0:
```python
import math

import jax
import jax.numpy as jnp
from jax import lax
from jax.sharding import PartitionSpec as P


def pack_rows(own_rows, send_rows, send_count):
    slot_total = send_rows.shape[2]
    picked = jnp.take(own_rows, send_rows[0].reshape(-1), axis=0)
    picked = picked.reshape(send_rows.shape[1], slot_total, own_rows.shape[1])
    in_use = jnp.arange(slot_total, dtype=jnp.int32)[None, :] < send_count[0][:, None]
    return jnp.where(in_use[:, :, None], picked, jnp.zeros_like(picked))


def aggregate(own_rows, arrived, tile_src, tile_val):
    col_count = own_rows.shape[1]
    blocks = jnp.concatenate([own_rows, arrived], axis=0).reshape(-1, 128, col_count)
    chosen = jnp.take(blocks, tile_src, axis=0)
    summed = jnp.einsum("bkij,bkjh->bih", tile_val, chosen, preferred_element_type=jnp.float32)
    return summed.reshape(own_rows.shape[0], col_count).astype(jnp.bfloat16)


def spread_back(grads, tile_src, tile_val, src_total):
    col_count = grads.shape[1]
    per_tile = jnp.einsum(
        "bkij,bih->bkjh",
        tile_val,
        grads.reshape(-1, 128, col_count),
        preferred_element_type=jnp.float32,
    )
    one_hot = (
        tile_src.reshape(-1)[None, :] == jnp.arange(src_total // 128, dtype=jnp.int32)[:, None]
    ).astype(jnp.float32)
    landed = jnp.dot(
        one_hot,
        per_tile.reshape(one_hot.shape[1], -1),
        precision=lax.Precision.HIGHEST,
        preferred_element_type=jnp.float32,
    )
    return landed.reshape(src_total, col_count)


def cross_entropy(logits, labels, grad_scale):
    row_max = jnp.max(logits, axis=1, keepdims=True)
    shifted = logits - row_max
    total_exp = jnp.sum(jnp.exp(shifted), axis=1, keepdims=True)
    classes = jnp.arange(logits.shape[1], dtype=jnp.int32)
    target = (labels[:, None] == classes[None, :]).astype(jnp.float32)
    row_loss = jnp.log(total_exp)[:, 0] - jnp.sum(shifted * target, axis=1)
    grads = ((jnp.exp(shifted) / total_exp - target) * grad_scale).astype(jnp.bfloat16)
    return (row_loss, grads)


def shards(
    features,
    send_rows,
    send_count,
    tile_src,
    tile_val,
    labels,
    w_self1,
    w_neigh1,
    w_self2,
    w_neigh2,
):
    node_count = lax.axis_size("node")
    own_count = features.shape[0]
    slot_total = send_rows.shape[2]
    src_total = own_count + node_count * slot_total
    node_total = own_count * node_count
    grad_scale = 1.0 / math.sqrt(node_total)
    outgoing = pack_rows(features, send_rows, send_count)
    arrived = lax.all_to_all(outgoing, "node", split_axis=0, concat_axis=0, tiled=True).reshape(
        -1, features.shape[1]
    )
    agg_one = aggregate(features, arrived, tile_src, tile_val)
    partial_one = jnp.dot(features, w_self1, preferred_element_type=jnp.float32)
    partial_one = partial_one + jnp.dot(agg_one, w_neigh1, preferred_element_type=jnp.float32)
    pre_act = lax.psum_scatter(partial_one, "feat", scatter_dimension=1, tiled=True)
    activated, pullback = jax.vjp(lambda inner: jax.nn.gelu(inner, approximate=True), pre_act)
    hidden = activated.astype(jnp.bfloat16)
    unit_count = hidden.shape[1]
    outgoing_two = pack_rows(hidden, send_rows, send_count)
    arrived_two = lax.all_to_all(
        outgoing_two, "node", split_axis=0, concat_axis=0, tiled=True
    ).reshape(-1, unit_count)
    agg_two = aggregate(hidden, arrived_two, tile_src, tile_val)
    partial_two = jnp.dot(hidden, w_self2, preferred_element_type=jnp.float32)
    partial_two = partial_two + jnp.dot(agg_two, w_neigh2, preferred_element_type=jnp.float32)
    logits = lax.psum(partial_two, "feat")
    row_loss, dlogits = cross_entropy(logits, labels, grad_scale)
    mean_loss = lax.psum(jnp.sum(row_loss), "node") / node_total
    grad_pair = lax.psum(
        (
            jnp.einsum("nh,nc->hc", hidden, dlogits, preferred_element_type=jnp.float32),
            jnp.einsum("nh,nc->hc", agg_two, dlogits, preferred_element_type=jnp.float32),
        ),
        "node",
    )
    back_grad = jnp.einsum(
        "nc,hc->nh", dlogits, w_neigh2, preferred_element_type=jnp.float32
    ).astype(jnp.bfloat16)
    direct = jnp.einsum("nc,hc->nh", dlogits, w_self2, preferred_element_type=jnp.float32)
    landed = spread_back(back_grad, tile_src, tile_val, src_total)
    halo_back = landed[own_count:].reshape(node_count, slot_total, unit_count)
    returned = lax.all_to_all(
        halo_back.astype(jnp.bfloat16), "node", split_axis=0, concat_axis=0, tiled=True
    ).astype(halo_back.dtype)
    in_use = jnp.arange(slot_total, dtype=jnp.int32)[None, :] < send_count[0][:, None]
    returned = jnp.where(in_use[:, :, None], returned, jnp.zeros_like(returned))
    back_rows = jax.ops.segment_sum(
        returned.reshape(-1, unit_count), send_rows[0].reshape(-1), num_segments=own_count
    )
    back_hidden = direct + landed[:own_count] + back_rows
    pre_grad = pullback(back_hidden)[0].astype(jnp.bfloat16)
    shard_piece = lax.all_gather(pre_grad, "feat", axis=1, tiled=True)
    local_grads = jnp.stack(
        [
            jnp.einsum("nf,nh->fh", features, shard_piece, preferred_element_type=jnp.float32),
            jnp.einsum("nf,nh->fh", agg_one, shard_piece, preferred_element_type=jnp.float32),
        ]
    )
    summed = lax.psum(local_grads, "node")
    return (mean_loss, summed[0], summed[1], grad_pair[0], grad_pair[1])


def solution(mesh):
    in_specs = (
        P("node", "feat"),
        P("node", None, None),
        P("node", None),
        P("node", None),
        P("node", None, None, None),
        P("node"),
        P("feat", None),
        P("feat", None),
        P("feat", None),
        P("feat", None),
    )
    out_specs = (P(), P("feat", None), P("feat", None), P("feat", None), P("feat", None))
    return jax.shard_map(shards, mesh=mesh, in_specs=in_specs, out_specs=out_specs, check_vma=False)
```

profile of v0, /device:TPU:1, one launch (start us, length us, event | category | flops | bytes accessed | tf_op | source)
XLA Modules:
  0.0 570.9 jit_solution(3139560621322994043)
XLA Ops:
  7.2 1.0 reshape_squeeze.7
  8.2 0.9 iota_compare_fusion.1
  9.1 0.9 copy.35
  10.0 12.1 %gather_fusion = bf16[4096,32]{1,0:T(8,128)(2,1)S(1)} fusion(bf16[512,32]{1,0:T(8,128)(2,1)S(1)} %copy.35, s32[4096]{0:T(1024)S(1)} %broadcast_clamp_fusion), kind=kCustom, calls=%fused_computation | custom fusion | bytes 540672 | tf_op jit(solution)/shard_map/jit(_take)/gather | solution.py:11
  22.1 1.1 copy.36
  23.3 1.2 fusion.30
  24.4 1.0 reshape.178
  25.4 13.2 %all-to-all-start = ((bf16[64,2,1024]{2,1,0:T(2,128)(2,1)}), bf16[64,2,1024]{2,1,0:T(2,128)(2,1)S(1)}, u32[]{:S(2)}, u32[]{:S(2)}) async-start(bf16[64,2,1024]{2,1,0:T(2,128)(2,1)} %reshape.178), calls=%async_computation | async-start | bytes 524288 | tf_op jit(solution)/shard_map/all_to_all | solution.py:75
  38.8 1.8 fusion.31
  40.6 10.0 %all-to-all-done = bf16[64,2,1024]{2,1,0:T(2,128)(2,1)S(1)} async-done(((bf16[64,2,1024]{2,1,0:T(2,128)(2,1)}), bf16[64,2,1024]{2,1,0:T(2,128)(2,1)S(1)}, u32[]{:S(2)}, u32[]{:S(2)}) %all-to-all-start) | async-done | bytes 262176 | tf_op jit(solution)/shard_map/all_to_all | solution.py:75
  52.4 0.8 fusion.11
  53.2 0.7 copy-done.3
  53.9 1.8 convolution_add_fusion
  55.7 29.1 %reduce-scatter.2.cloned.1.call-done = f32[512,256]{1,0:T(8,128)} async-done(((f32[512,1024]{1,0:T(8,128)}), f32[512,256]{1,0:T(8,128)}) %reduce-scatter.2.cloned.1.call-update) | async-done | bytes 524304 | tf_op jit(solution)/shard_map/reduce_scatter | solution.py:81
  84.8 1.2 multiply_convert_fusion
  86.0 16.9 %gather_fusion.2 = bf16[4096,256]{1,0:T(8,128)(2,1)} fusion(bf16[512,256]{1,0:T(8,128)(2,1)S(1)} %multiply_convert_fusion, s32[4096]{0:T(1024)S(1)} %broadcast_clamp_fusion), kind=kCustom, calls=%fused_computation.2 | custom fusion | bytes 4210688 | tf_op jit(solution)/shard_map/jit(_take)/gather | solution.py:11
  102.9 4.4 select_select_fusion
  107.3 11.0 %all-to-all-start.1 = ((bf16[64,64,256]{2,1,0:T(8,128)(2,1)}), bf16[64,64,256]{2,1,0:T(8,128)(2,1)}, u32[]{:S(2)}, u32[]{:S(2)}) async-start(bf16[64,64,256]{2,1,0:T(8,128)(2,1)} %select_select_fusion), calls=%async_computation.2 | async-start | bytes 4194304 | tf_op jit(solution)/shard_map/all_to_all | solution.py:86
  118.6 50.9 %all-to-all-done.1 = bf16[64,64,256]{2,1,0:T(8,128)(2,1)} async-done(((bf16[64,64,256]{2,1,0:T(8,128)(2,1)}), bf16[64,64,256]{2,1,0:T(8,128)(2,1)}, u32[]{:S(2)}, u32[]{:S(2)}) %all-to-all-start.1) | async-done | bytes 2097184 | tf_op jit(solution)/shard_map/all_to_all | solution.py:86
  169.5 3.2 pad_maximum_fusion
  172.7 4.4 gather_fusion.3
  177.1 3.2 fusion.7
  180.3 1.0 convolution_add_fusion.2
  181.4 40.0 %all-reduce.4.cloned.1.call-done = f32[512,172]{0,1:T(8,128)} async-done(((f32[512,172]{0,1:T(8,128)}), f32[512,172]{0,1:T(8,128)}) %all-reduce.4.cloned.1.call-update) | async-done | bytes 352272 | tf_op jit(solution)/shard_map/psum | solution.py:92
  221.4 1.0 reduce_max.9
  222.4 1.1 exponential_reduce_fusion
  223.5 1.1 multiply_convert_fusion.1
  224.9 4.5 convolution_bitcast_fusion
  229.4 8.7 %copy.41 = f32[4,16,128,256]{3,2,1,0:T(8,128)} copy(f32[4,16,128,256]{2,3,1,0:T(8,128)} %convolution_bitcast_fusion) | data formatting | bytes 16777216 | tf_op jit(solution)/shard_map/bkij,bih->bkjh/dot_general | solution.py:27
  238.1 8.1 %copy.49 = f32[8,8,128,256]{3,1,2,0:T(8,128)S(1)} copy(f32[8,8,128,256]{3,2,1,0:T(8,128)} %bitcast.90) | data formatting | bytes 16777216
  246.2 4.3 fusion.26
  250.5 2.3 copy-done.2
  253.2 2.4 convert_element_type.51
  255.6 13.1 %all-to-all-start.2 = ((bf16[64,64,256]{2,1,0:T(8,128)(2,1)}), bf16[64,64,256]{2,1,0:T(8,128)(2,1)}, u32[]{:S(2)}, u32[]{:S(2)}) async-start(bf16[64,64,256]{2,1,0:T(8,128)(2,1)} %convert_element_type.51), calls=%async_computation.3 | async-start | bytes 4194304 | tf_op jit(solution)/shard_map/all_to_all | solution.py:108
  269.5 50.4 %all-to-all-done.2 = bf16[64,64,256]{2,1,0:T(8,128)(2,1)} async-done(((bf16[64,64,256]{2,1,0:T(8,128)(2,1)}), bf16[64,64,256]{2,1,0:T(8,128)(2,1)}, u32[]{:S(2)}, u32[]{:S(2)}) %all-to-all-start.2) | async-done | bytes 2097184 | tf_op jit(solution)/shard_map/all_to_all | solution.py:108
  319.9 3.5 convert_select_fusion
  323.4 23.3 %scatter_fusion = f32[512,256]{1,0:T(8,128)S(1)} fusion(f32[512,256]{1,0:T(8,128)S(1)} %convolution_add_fusion.1, s32[4096]{0:T(1024)S(1)} %reshape.164, f32[4096,256]{1,0:T(8,128)} %bitcast.92), kind=kCustom, calls=%fused_computation.4 | custom fusion | flops 1048576 | bytes 12599296 | tf_op jit(solution)/shard_map/scatter-add | solution.py:113
  346.7 1.1 fusion.18
  347.9 0.9 fusion.34
  348.8 0.9 fusion.33
  349.6 21.5 %all-gather.2.cloned.1.call-done = bf16[512,1024]{1,0:T(8,128)(2,1)} async-done(((bf16[512,256]{1,0:T(8,128)(2,1)}), bf16[512,1024]{1,0:T(8,128)(2,1)}) %all-gather.2.cloned.1.call-update) | async-done | bytes 1048592 | tf_op jit(solution)/shard_map/all_gather | solution.py:118
  371.2 1.7 convolution_bitcast_fusion.2
  372.8 1.5 convolution_bitcast_fusion.1
  375.7 126.2 %psum.36 = f32[]{:T(128)} all-reduce(f32[]{:T(128)} %subtract_reduce_fusion), channel_id=1, replica_groups=mesh['node'=64,'feat'=4] {'node'}, use_global_device_ids=true, to_apply=%region_6.7 | all-reduce | flops 1 | bytes 8 | tf_op jit(solution)/shard_map/psum | solution.py:94
  502.5 55.9 %all-reduce.6.cloned.1.call-done = (f32[2,32,1024]{2,1,0:T(8,128)}, f32[256,172]{0,1:T(8,128)}, f32[256,172]{0,1:T(8,128)}) async-done(((f32[2,32,1024]{2,1,0:T(8,128)}, f32[256,172]{0,1:T(8,128)}, f32[256,172]{0,1:T(8,128)}), (f32[2,32,1024]{2,1,0:T(8,128)}, f32[256,172]{0,1:T(8,128)}, f32[256,172]{0,1:T(8,128)})) %all-reduce.6.cloned.1.call-update) | async-done | bytes 614416 | tf_op jit(solution)/shard_map/psum | solution.py:125
  558.4 1.7 slice_bitcast_fusion
  560.0 1.6 copy.64
  561.7 1.6 copy.65
  (54 shorter events, 5.1 us)
Async XLA Ops:
  7.2 45.2 %copy-start = (bf16[4,16,128,128]{3,2,1,0:T(8,128)(2,1)S(1)}, bf16[4,16,128,128]{3,2,1,0:T(8,128)(2,1)}, u32[]{:S(2)}) copy-start(bf16[4,16,128,128]{3,2,1,0:T(8,128)(2,1)} %param.14) | copy-start | bytes 6291460
  22.1 16.5 %copy-start.11 = (s32[4,16]{1,0:T(4,128)S(1)}, s32[4,16]{1,0:T(4,128)}, u32[]{:S(2)}) copy-start(s32[4,16]{1,0:T(4,128)} %param.13) | copy-start | bytes 772
  22.1 16.7 %copy-start.5 = (bf16[512,32]{0,1:T(8,128)(2,1)S(1)}, bf16[512,32]{0,1:T(8,128)(2,1)}, u32[]{:S(2)}) copy-start(bf16[512,32]{0,1:T(8,128)(2,1)} %param.10) | copy-start | bytes 98308
  22.1 16.7 %copy-start.10 = (bf16[32,1024]{1,0:T(8,128)(2,1)S(1)}, bf16[32,1024]{1,0:T(8,128)(2,1)}, u32[]{:S(2)}) copy-start(bf16[32,1024]{1,0:T(8,128)(2,1)} %param.16) | copy-start | bytes 196612
  25.4 25.2 %all-to-all-start = ((bf16[64,2,1024]{2,1,0:T(2,128)(2,1)}), bf16[64,2,1024]{2,1,0:T(2,128)(2,1)S(1)}, u32[]{:S(2)}, u32[]{:S(2)}) async-start(bf16[64,2,1024]{2,1,0:T(2,128)(2,1)} %reshape.178), calls=%async_computation | async-start | bytes 524288 | tf_op jit(solution)/shard_map/all_to_all | solution.py:75
  38.6 46.2 %reduce-scatter.2.cloned.1.call-start = ((), (), s32[]{:S(2)}) async-start(), calls=%async_computation.4 | async-start | bytes 2621440 | tf_op jit(solution)/shard_map/reduce_scatter | solution.py:81
  52.3 1.6 copy-start.3
  52.3 1.6 copy-start.9
  107.3 11.0 %copy-start.7 = (bf16[256,172]{0,1:T(8,128)(2,1)S(1)}, bf16[256,172]{0,1:T(8,128)(2,1)}, u32[]{:S(2)}) copy-start(bf16[256,172]{0,1:T(8,128)(2,1)} %param.18) | copy-start | bytes 264196
  107.3 62.1 %all-to-all-start.1 = ((bf16[64,64,256]{2,1,0:T(8,128)(2,1)}), bf16[64,64,256]{2,1,0:T(8,128)(2,1)}, u32[]{:S(2)}, u32[]{:S(2)}) async-start(bf16[64,64,256]{2,1,0:T(8,128)(2,1)} %select_select_fusion), calls=%async_computation.2 | async-start | bytes 4194304 | tf_op jit(solution)/shard_map/all_to_all | solution.py:86
  118.3 103.1 %all-reduce.4.cloned.1.call-start = ((), (), s32[]{:S(2)}) async-start(), calls=%async_computation.5 | async-start | bytes 720896 | tf_op jit(solution)/shard_map/psum | solution.py:92
  177.1 3.2 copy-start.6
  177.1 45.4 %copy-start.12 = (s32[512]{0:T(512)S(1)}, s32[512]{0:T(512)}, u32[]{:S(2)}) copy-start(s32[512]{0:T(512)} %param.15) | copy-start | bytes 6148
  250.5 2.3 copy-start.2
  255.6 13.2 %copy-start.8 = (s32[1,64,64]{2,1,0:T(8,128)S(1)}, s32[1,64,64]{2,1,0:T(8,128)}, u32[]{:S(2)}) copy-start(s32[1,64,64]{2,1,0:T(8,128)} %param.11) | copy-start | bytes 49156
  255.6 13.3 %slice-start = ((f32[36,32768]{1,0:T(8,128)}), f32[4,32768]{1,0:T(4,128)S(1)}, s32[]{:S(2)}) async-start(f32[36,32768]{1,0:T(8,128)} %copy-done.2), calls=%async_computation.8 | async-start | bytes 1048576 | tf_op jit(solution)/shard_map/slice | solution.py:116
  255.6 64.3 %all-to-all-start.2 = ((bf16[64,64,256]{2,1,0:T(8,128)(2,1)}), bf16[64,64,256]{2,1,0:T(8,128)(2,1)}, u32[]{:S(2)}, u32[]{:S(2)}) async-start(bf16[64,64,256]{2,1,0:T(8,128)(2,1)} %convert_element_type.51), calls=%async_computation.3 | async-start | bytes 4194304 | tf_op jit(solution)/shard_map/all_to_all | solution.py:108
  268.8 102.4 %all-gather.2.cloned.1.call-start = ((), (), s32[]{:S(2)}) async-start(), calls=%async_computation.6 | async-start | bytes 1310720 | tf_op jit(solution)/shard_map/all_gather | solution.py:118
  323.4 23.3 %copy-start.4 = (f32[512,256]{1,0:T(8,128)S(1)}, f32[512,256]{1,0:T(8,128)}, u32[]{:S(2)}) copy-start(f32[512,256]{1,0:T(8,128)} %reduce-scatter.2.cloned.1.call-done) | copy-start | bytes 1572868
  347.8 210.5 %all-reduce.6.cloned.1.call-start = ((), (), s32[]{:S(2)}) async-start(), calls=%async_computation.7 | async-start | bytes 1245184 | tf_op jit(solution)/shard_map/psum | solution.py:125
  371.1 192.1 %copy-start.1 = (bf16[4,16,128,128]{3,2,1,0:T(8,128)(2,1)S(1)}, bf16[4,16,128,128]{3,2,1,0:T(8,128)(2,1)}, u32[]{:S(2)}) copy-start(bf16[4,16,128,128]{3,2,1,0:T(8,128)(2,1)} %param.14) | copy-start | bytes 6291460
Sparse Core Ops, SparseCore 0:
  55.9 28.9 reduce-scatter.1
  181.5 39.9 all-reduce.3
  347.9 23.1 all-gather.1
  375.8 182.4 all-reduce.5
where the time goes:
time: 572 us; the launch traced here: 571 us
  waiting for transfers between devices  258 us (45%)
  blocking collectives  126 us (22%)
  local copies, waits for them, and re-layouts  67.3 us (12%)
  other arithmetic  43.3 us (8%)
  starting transfers between devices  37.4 us (7%)
  matrix products  23.1 us (4%)
  between operations  15.8 us (3%)
    psum x1, blocking collectives, shards(): mean_loss = lax.psum(jnp.sum(row_loss), 'node') / node_total  126 us
    psum x1, waiting for transfers between devices, shards(): summed = lax.psum(local_grads, 'node')  55.9 us
    all_to_all x1, waiting for transfers between devices, shards(): lax.all_to_all(outgoing_two, 'node', split_axis=0, concat_axis=0, tiled=T...  50.9 us
    all_to_all x1, waiting for transfers between devices, shards(): lax.all_to_all(halo_back.astype(jnp.bfloat16), 'node', split_axis=0, conc...  50.4 us
    psum x1, waiting for transfers between devices, shards(): logits = lax.psum(partial_two, 'feat')  40 us
    gather x3, local copies, waits for them, and re-layouts, pack_rows(): picked = jnp.take(own_rows, send_rows[0].reshape(-1), axis=0)  30.2 us
    reduce_scatter x1, waiting for transfers between devices, shards(): lax.psum_scatter(partial_one, 'feat', scatter_dimension=1, tiled=True)  29.1 us
    scatter-add x1, other arithmetic, shards(): jax.ops.segment_sum(returned.reshape(-1, unit_count), send_rows[0].reshap...  23.3 us
  transfers between devices with their start and end apart: 7, of which 7 were waited for; matrix products, arithmetic and copies ran while one was open for 1% of the time, Pallas kernels for 0%

commit v1 on v0

v1 whole, which is shorter than its diff:
```python
import functools
import math

import jax
import jax.numpy as jnp
from jax import lax
from jax.experimental import pallas as pl
from jax.experimental.pallas import tpu as pltpu
from jax.sharding import PartitionSpec as P

MESH = pl.DeviceIdType.MESH
F32 = jnp.float32
BF = jnp.bfloat16
ROWS = 512
SLOTS = 64
NODES = 64
FEATS = 4
CHIPS = NODES // 2
TILES = 64
BLOCKS = 36
CLS = 43
GELU_C = math.sqrt(2.0 / math.pi)


def g1_row(chip):
    y, z = chip // 8, chip % 8
    keep = (y + z) % 4
    rt = y * 2 + z // 4
    return (rt // 4) * 128 + 32 * keep + 8 * (rt % 4), keep, rt


def lane_roll(value, shift):
    shift = shift % value.shape[-1]
    return pltpu.roll(value, shift, value.ndim - 1) if shift else value


def dot(a, b):
    return jnp.dot(a, b, preferred_element_type=F32)


def step_kernel(
    grad_scale,
    table, xcat, slot_col, slot_row, tiles, labels, w1s, w1n, w2p,
    loss_ref, ogs1_ref, ogn1_ref, ogs2_ref, ogn2_ref,
    hot, hot_t, tiles_t, src, run, ptile,
    out1, recv1, xrecv, w1s_full, w1n_full, aggp, agg_recv, xfull, aggf,
    slope, hid, hid_t, xa_t, pf, ycat, ypack, yown, yrecv, spack, srecv,
    out2, recv2, stat, dlp, ret, recvb, gp, dg,
    dpart, dpeer, dsum, rrecv, rtile, trecv, fin01, fin2, half01, half2,
    s_x, r_x, s_w, r_w, s_e1, r_e1, s_agg, r_agg, s_y, r_y, s_s, r_s, s_e2, r_e2,
    s_st, r_st, s_dl, r_dl, s_eb, r_eb, s_g, r_g, s_d, r_d, s_rs, r_rs,
    s_t, r_t, s_f, r_f, s_f2, r_f2, s_h, r_h, s_h2, r_h2,
):
    me = lax.axis_index("node")
    f = lax.axis_index("feat")
    chip, core = me // 2, me % 2
    partner = me + 1 - 2 * core

    def wait_bytes(ref, sem):
        pltpu.make_async_copy(ref, ref, sem).wait()

    def send(s, d, ssem, rsem, node, feat):
        pltpu.make_async_remote_copy(
            src_ref=s, dst_ref=d, send_sem=ssem, recv_sem=rsem,
            device_id=(node, feat), device_id_type=MESH,
        ).start()

    def to_nodes(s, d, ssem, rsem):
        def body(i, c):
            p = lax.rem(me + i, NODES)
            send(s.at[p], d.at[me], ssem, rsem, p, f)
            return c
        lax.fori_loop(1, NODES, body, 0)

    def to_feats(s, d, ssem, rsem, same=False):
        for i in range(1, FEATS):
            g = lax.rem(f + i, FEATS)
            send(s if same else s.at[g], d.at[f], ssem, rsem, me, g)

    lane = lambda r, n=128: lax.broadcasted_iota(jnp.int32, (r, n), 1)

    bar = pltpu.get_barrier_semaphore()

    def hello(i, c):
        pl.semaphore_signal(bar, inc=1, device_id=(lax.rem(me + i, NODES), f), device_id_type=MESH)
        return c

    lax.fori_loop(1, NODES, hello, 0)
    for i in range(1, FEATS):
        pl.semaphore_signal(bar, inc=1, device_id=(me, lax.rem(f + i, FEATS)), device_id_type=MESH)

    def build_hot(d, c):
        col = jnp.sum(jnp.where(lane(SLOTS) == d, slot_col[...], 0), axis=1, keepdims=True)
        hot[d] = jnp.where(col == lane(SLOTS, ROWS), 1.0, 0.0).astype(BF)
        return c

    lax.fori_loop(0, NODES, build_hot, 0)

    def pack1(m, c):
        d0 = pl.multiple_of(m * 32, 32)
        acc = jnp.zeros((ROWS, 128), F32)
        for q in range(4):
            sel = hot[pl.ds(d0, 32), 16 * q:16 * q + 16, :].reshape(512, ROWS)
            acc = acc + dot(sel, xcat[q])
        out1[pl.ds(d0, 32)] = acc.astype(BF).reshape(32, 16, 128)
        return c

    lax.fori_loop(0, 2, pack1, 0)
    pl.semaphore_wait(bar, NODES - 1 + FEATS - 1)

    to_nodes(out1, recv1, s_e1, r_e1)
    for i in range(1, FEATS):
        g = lax.rem(f + i, FEATS)
        send(xcat.at[f], xrecv.at[f], s_x, r_x, me, g)
        send(w1s.at[g], w1s_full.at[f], s_w.at[0], r_w.at[0], me, g)
        send(w1n.at[g], w1n_full.at[f], s_w.at[1], r_w.at[1], me, g)

    recv1[me] = out1[me]
    xrecv[f] = xcat[f]
    w1s_full[f] = w1s[f]
    w1n_full[f] = w1n[f]
    for b in range(4):
        src[b] = xcat[0, 128 * b:128 * b + 128, :]

    def turn(t, c):
        tiles_t[t] = jnp.transpose(tiles[t])
        return c

    lax.fori_loop(0, TILES, turn, 0)

    def build_hot_t(m, c):
        r0 = pl.multiple_of(m * 64, 64)
        rows = lax.broadcasted_iota(jnp.int32, (64, 2048), 0) + r0
        for h in range(2):
            hot_t[h, pl.ds(r0, 64), :] = jnp.where(rows == slot_row[h:h + 1, :], 1.0, 0.0).astype(BF)
        return c

    lax.fori_loop(0, 8, build_hot_t, 0)

    wait_bytes(recv1.at[pl.ds(0, NODES - 1)], r_e1)

    def unpack1(j, c):
        for p in range(2):
            v = recv1[2 * j + p].astype(F32)
            for q in range(4):
                src[4 + j, 64 * p + 16 * q:64 * p + 16 * q + 16, :] = lane_roll(v, -32 * q).astype(BF)
        return c

    lax.fori_loop(0, 32, unpack1, 0)

    def tile_product(b):
        lhs = jnp.concatenate([tiles[16 * b + k] for k in range(16)], axis=1)
        rhs = jnp.concatenate([src[table[16 * b + k]] for k in range(16)], axis=0)
        return dot(lhs, rhs)

    packed = jnp.zeros((128, 128), F32)
    group = lane(128) // 32
    for b in range(4):
        packed = packed + lane_roll(jnp.where(group == 0, tile_product(b), 0.0), 32 * b)
    aggp[...] = packed.astype(BF)
    to_feats(aggp, agg_recv, s_agg, r_agg, same=True)
    agg_recv[f] = aggp[...]

    wait_bytes(xrecv.at[pl.ds(0, FEATS - 1)], r_x)
    wait_bytes(w1s_full.at[pl.ds(0, FEATS - 1)], r_w.at[0])
    wait_bytes(w1n_full.at[pl.ds(0, FEATS - 1)], r_w.at[1])
    xf = xrecv[0] + xrecv[1] + xrecv[2] + xrecv[3]
    xfull[...] = xf
    wait_bytes(agg_recv.at[pl.ds(0, FEATS - 1)], r_agg)
    for b in range(4):
        acc = jnp.zeros((128, 128), F32)
        for g in range(4):
            acc = jnp.where(group == g, lane_roll(agg_recv[g].astype(F32), 32 * (g - b)), acc)
        aggf[128 * b:128 * b + 128, :] = acc.astype(BF)

    pre = dot(xfull[...], w1s_full[...].reshape(128, 256)) + dot(aggf[...], w1n_full[...].reshape(128, 256))
    th = jnp.tanh(GELU_C * (pre + 0.044715 * (pre * pre * pre)))
    cdf = 0.5 * (1.0 + th)
    slope[...] = cdf + pre * (0.5 * (1.0 - th * th)) * (GELU_C * (1.0 + 3.0 * 0.044715 * (pre * pre)))
    hid[...] = (pre * cdf).astype(BF)

    low256 = lane(256) < 64
    for g in range(4):
        v = dot(hid[...], w2p[:, 128 * g:128 * g + 128])
        va, vb = v[0:256], v[256:512]
        yv = jnp.where(low256, lane_roll(va, 64), vb)
        yown[g] = yv
        ypack[g] = yv.astype(BF)
        spack[g] = jnp.where(low256, va, lane_roll(vb, 64))
    to_feats(ypack, yrecv, s_y, r_y)
    to_feats(spack, srecv, s_s, r_s)
    yrecv[f] = jnp.zeros((256, 128), BF)
    srecv[f] = spack[f]
    wait_bytes(yrecv.at[pl.ds(0, FEATS - 1)], r_y)
    ys = yown[f]
    for g in range(4):
        ys = ys + yrecv[g].astype(F32)
    yr = lane_roll(ys, 64)
    ycat[0, 0:256, :] = jnp.where(low256, ys, 0.0).astype(BF)
    ycat[0, 256:512, :] = jnp.where(low256, yr, 0.0).astype(BF)
    ycat[1, 0:256, :] = jnp.where(low256, 0.0, yr).astype(BF)
    ycat[1, 256:512, :] = jnp.where(low256, 0.0, ys).astype(BF)

    def pack2(m, c):
        d0 = pl.multiple_of(m * 16, 16)
        acc = dot(hot[pl.ds(d0, 16), 0:32, :].reshape(512, ROWS), ycat[0])
        acc = acc + dot(hot[pl.ds(d0, 16), 32:64, :].reshape(512, ROWS), ycat[1])
        out2[pl.ds(d0, 16)] = acc.astype(BF).reshape(16, 32, 128)
        return c

    lax.fori_loop(0, 4, pack2, 0)
    to_nodes(out2, recv2, s_e2, r_e2)

    recv2[me] = out2[me]
    for b in range(4):
        src[b] = ycat[0, 128 * b:128 * b + 128, :]
    hid_t[...] = jnp.transpose(hid[...])
    xa_t[0:128, :] = jnp.transpose(xfull[...])
    xa_t[128:256, :] = jnp.transpose(aggf[...])

    wait_bytes(recv2.at[pl.ds(0, NODES - 1)], r_e2)

    def unpack2(j, c):
        for p in range(2):
            v = recv2[2 * j + p]
            src[4 + j, 64 * p:64 * p + 32, :] = v
            src[4 + j, 64 * p + 32:64 * p + 64, :] = lane_roll(v.astype(F32), 64).astype(BF)
        return c

    lax.fori_loop(0, 32, unpack2, 0)

    wait_bytes(srecv.at[pl.ds(0, FEATS - 1)], r_s)
    ss = srecv[0] + srecv[1] + srecv[2] + srecv[3]
    pf[0, 0:256, :] = ss
    pf[0, 256:512, :] = lane_roll(ss, 64)

    mine = lane(128) < CLS
    lane128 = lane(128)
    for b in range(4):
        r = slice(128 * b, 128 * b + 128)
        lg = jnp.where(mine, pf[0, r, :] + tile_product(b), -1e30)
        top = jnp.max(lg, axis=1, keepdims=True)
        ex = jnp.exp(lg - top)
        tot = jnp.sum(ex, axis=1, keepdims=True)
        want = mine & ((labels[r, :] - CLS * f) == lane128)
        hit = jnp.sum(jnp.where(want, lg, 0.0), axis=1, keepdims=True)
        st = jnp.where(lane128 == 0, top, jnp.where(lane128 == 1, tot, jnp.where(lane128 == 2, hit, 0.0)))
        stat[f, :, r] = jnp.transpose(st)[0:8, :]
        pf[1, r, :] = ex
        pf[2, r, :] = jnp.where(want, 1.0, 0.0)
    to_feats(stat.at[f], stat, s_st, r_st, same=True)
    wait_bytes(stat.at[pl.ds(0, FEATS - 1)], r_st)

    tops = [stat[g, 0:1, :] for g in range(4)]
    best = jnp.maximum(jnp.maximum(tops[0], tops[1]), jnp.maximum(tops[2], tops[3]))
    total = jnp.zeros_like(best)
    hits = jnp.zeros_like(best)
    for g in range(4):
        total = total + stat[g, 1:2, :] * jnp.exp(tops[g] - best)
        hits = hits + stat[g, 2:3, :]
    loss = jnp.sum(jnp.log(total) + best - hits)
    factor = jnp.exp(stat[f, 0:1, :] - best) / total
    factor = jnp.broadcast_to(factor, (128, ROWS))
    for b in range(4):
        r = slice(128 * b, 128 * b + 128)
        fac = jnp.transpose(factor[:, 128 * b:128 * b + 128])
        d = (pf[1, r, :] * fac - pf[2, r, :]) * grad_scale
        dl = d.astype(BF)
        hi = b // 2
        rows = slice(128 * (b % 2), 128 * (b % 2) + 128)
        if hi == 0:
            dlp[f, rows, :] = dl
        else:
            dlp[f, rows, :] = (dlp[f, rows, :].astype(F32) + lane_roll(dl.astype(F32), 64)).astype(BF)
        lhs = tiles_t[16 * b:16 * b + 16].reshape(2048, 128)
        ptile[16 * b:16 * b + 16] = dot(lhs, dl).reshape(16, 128, 128)
    to_feats(dlp.at[f], dlp, s_dl, r_dl, same=True)

    def gather_sum(t, acc):
        keep = table[128 + t].astype(F32)
        acc = acc * keep + ptile[table[64 + t]]
        run[t] = acc
        return acc

    lax.fori_loop(0, TILES, gather_sum, jnp.zeros((128, 128), F32))

    def landed(j):
        return run[table[192 + j]] * table[256 + j].astype(F32)

    def pack_back(j, c):
        blk = landed(4 + j)
        for p in range(2):
            v = blk[64 * p:64 * p + 32, :] + lane_roll(blk[64 * p + 32:64 * p + 64, :], 64)
            ret[2 * j + p] = v.astype(BF)
        return c

    lax.fori_loop(0, 32, pack_back, 0)
    to_nodes(ret, recvb, s_eb, r_eb)
    recvb[me] = ret[me]
    for b in range(4):
        pf[3, 128 * b:128 * b + 128, :] = landed(b)

    wait_bytes(recvb.at[pl.ds(0, NODES - 1)], r_eb)
    back = recvb[...].reshape(2048, 128)
    low = lane(ROWS) < 64
    g_sum = pf[3] + jnp.where(low, dot(hot_t[0], back), 0.0)
    g_sum = g_sum + jnp.where(low, lane_roll(dot(hot_t[1], back), 64), 0.0)
    gp[f] = (g_sum[0:256] + lane_roll(g_sum[256:512], 64)).astype(BF)
    to_feats(gp.at[f], gp, s_g, r_g, same=True)
    wait_bytes(dlp.at[pl.ds(0, FEATS - 1)], r_dl)
    wait_bytes(gp.at[pl.ds(0, FEATS - 1)], r_g)
    for g in range(4):
        a, b = dlp[g].astype(F32), gp[g].astype(F32)
        dg[0:256, 128 * g:128 * g + 128] = jnp.where(low256, a, lane_roll(b, 64)).astype(BF)
        dg[256:512, 128 * g:128 * g + 128] = jnp.where(low256, lane_roll(a, 64), b).astype(BF)

    bh = lax.dot_general(dg[...], w2p[...], (((1,), (1,)), ((), ())), preferred_element_type=F32)
    bp = (bh * slope[...]).astype(BF)
    g1 = dot(xa_t[...], bp)
    g2 = dot(hid_t[...], dg[...])
    lane2 = lane(256, 256)
    zero = jnp.zeros((256, 128), F32)
    first = (lax.broadcasted_iota(jnp.int32, (256, 256), 0) == 0) & (lane2 == 255)
    gs2 = jnp.where(first, loss, 0.0)
    gn2 = jnp.zeros((256, 256), F32)
    l1 = lane(256)
    for g in range(4):
        blk = g2[:, 128 * g:128 * g + 128]
        s_part = jnp.concatenate([jnp.where(l1 < CLS, blk, 0.0), zero], axis=1)
        n_part = jnp.concatenate([jnp.where(l1 < 64, 0.0, blk), zero], axis=1)
        gs2 = gs2 + lane_roll(s_part, CLS * g)
        gn2 = gn2 + lane_roll(n_part, CLS * g - 64)
    for l in range(2):
        c = slice(128 * l, 128 * l + 128)
        dpart[l, :, 0] = gs2[:, c].reshape(CHIPS, 8, 128)
        dpart[l, :, 1] = gn2[:, c].reshape(CHIPS, 8, 128)
        for ch in range(CHIPS):
            r0 = g1_row(ch)[0]
            dpart[l, ch, 2] = g1[r0:r0 + 8, c]

    send(dpart.at[1 - core], dpeer, s_d, r_d, partner, f)
    wait_bytes(dpeer, r_d)
    dsum[...] = dpart[core] + dpeer[...]

    def scatter(i, c):
        p = lax.rem(chip + i, CHIPS)
        send(dsum.at[p], rrecv.at[chip], s_rs, r_rs, 2 * p + core, f)
        return c

    lax.fori_loop(1, CHIPS, scatter, 0)
    rrecv[chip] = dsum[chip]
    wait_bytes(rrecv.at[pl.ds(0, CHIPS - 1)], r_rs)
    rtile[...] = jnp.sum(rrecv[...], axis=0)

    y, z = chip // 8, lax.rem(chip, 8)
    keep = lax.rem(y + z, 4)
    rt = y * 2 + z // 4
    mine_keep = keep == f

    @pl.when(jnp.logical_not(mine_keep))
    def _():
        send(rtile.at[2], trecv.at[f], s_t, r_t, me, keep)

    def spread01(i, c):
        p = lax.rem(chip + i, CHIPS)
        send(rtile.at[pl.ds(0, 2)], fin01.at[chip], s_f, r_f, 2 * p + core, f)
        return c

    lax.fori_loop(1, CHIPS, spread01, 0)
    fin01[chip] = rtile[0:2]

    @pl.when(mine_keep)
    def _():
        trecv[f] = rtile[2]
        wait_bytes(trecv.at[pl.ds(0, FEATS - 1)], r_t)

        def spread2(i, c):
            p = lax.rem(chip + i, CHIPS)
            send(trecv, fin2.at[rt], s_f2, r_f2, 2 * p + core, f)
            return c

        lax.fori_loop(1, CHIPS, spread2, 0)
        fin2[rt] = trecv[...]
        wait_bytes(fin2.at[pl.ds(0, 7)], r_f2)

    @pl.when(jnp.logical_not(mine_keep))
    def _():
        wait_bytes(fin2, r_f2)

    send(fin2, half2, s_h2, r_h2, partner, f)
    wait_bytes(fin01.at[pl.ds(0, CHIPS - 1)], r_f)
    send(fin01, half01, s_h, r_h, partner, f)

    def emit(l, a01, a2):
        for blk, ref in ((0, ogs2_ref), (1, ogn2_ref)):
            v = a01[:, blk].reshape(256, 128)
            if l == 0:
                ref[:, 0:128] = v
            else:
                ref[:, 128:172] = v[:, 0:44]
                if blk == 0:
                    loss_ref[...] = v[0:8, :]
        for g in range(4):
            cols = slice(256 * g + 128 * l, 256 * g + 128 * l + 128)
            ogs1_ref[:, cols] = a2[0:4, g].reshape(32, 128)
            ogn1_ref[:, cols] = a2[4:8, g].reshape(32, 128)

    @pl.when(core == 0)
    def _():
        emit(0, fin01[...], fin2[...])

    @pl.when(core == 1)
    def _():
        emit(1, fin01[...], fin2[...])

    wait_bytes(half2, r_h2)
    wait_bytes(half01, r_h)

    @pl.when(core == 0)
    def _():
        emit(1, half01[...], half2[...])

    @pl.when(core == 1)
    def _():
        emit(0, half01[...], half2[...])

    n63, f3, c31 = pl.ds(0, NODES - 1), pl.ds(0, FEATS - 1), pl.ds(0, CHIPS - 1)
    wait_bytes(recv1.at[n63], s_e1)
    wait_bytes(xrecv.at[f3], s_x)
    wait_bytes(w1s_full.at[f3], s_w.at[0])
    wait_bytes(w1n_full.at[f3], s_w.at[1])
    wait_bytes(agg_recv.at[f3], s_agg)
    wait_bytes(yrecv.at[f3], s_y)
    wait_bytes(srecv.at[f3], s_s)
    wait_bytes(recv2.at[n63], s_e2)
    wait_bytes(stat.at[f3], s_st)
    wait_bytes(dlp.at[f3], s_dl)
    wait_bytes(recvb.at[n63], s_eb)
    wait_bytes(gp.at[f3], s_g)
    wait_bytes(dpeer, s_d)
    wait_bytes(rrecv.at[c31], s_rs)
    wait_bytes(fin01.at[c31], s_f)
    wait_bytes(half2, s_h2)
    wait_bytes(half01, s_h)

    @pl.when(jnp.logical_not(mine_keep))
    def _():
        wait_bytes(trecv.at[0], s_t)

    @pl.when(mine_keep)
    def _():
        wait_bytes(ptile.at[pl.ds(0, CHIPS - 1), pl.ds(0, 32)], s_f2)


def tile_table(tile_src):
    src = tile_src.reshape(-1)
    spot = jnp.arange(TILES, dtype=jnp.int32)
    before = (src[None, :] < src[:, None]) | ((src[None, :] == src[:, None]) & (spot[None, :] < spot[:, None]))
    rank = jnp.sum(before.astype(jnp.int32), axis=1)
    at = rank[:, None] == spot[None, :]
    order = jnp.sum(jnp.where(at, spot[:, None], 0), axis=0)
    same = (src[None, :] == src[:, None]) & (spot[None, :] < spot[:, None])
    goes_on_own = jnp.any(same, axis=1).astype(jnp.int32)
    goes_on = jnp.sum(jnp.where(at, goes_on_own[:, None], 0), axis=0)
    block = jnp.arange(TILES, dtype=jnp.int32)
    last = jnp.maximum(jnp.sum((src[None, :] <= block[:, None]).astype(jnp.int32), axis=1) - 1, 0)
    filled = jnp.any(src[None, :] == block[:, None], axis=1).astype(jnp.int32)
    return jnp.concatenate([src, order, goes_on, last, filled])


def shards(features, send_rows, send_count, tile_src, tile_val, labels, w_self1, w_neigh1, w_self2, w_neigh2):
    grad_scale = 1.0 / math.sqrt(ROWS * NODES)
    used = jnp.arange(SLOTS, dtype=jnp.int32)[None, :] < send_count[0][:, None]
    slots = jnp.where(used, send_rows[0], -1)
    slot_col = jnp.pad(slots.T, ((0, 0), (0, 64)))
    slot_row = slots.reshape(NODES, 2, 32).transpose(1, 0, 2).reshape(2, 2048)
    xcat = jnp.stack([jnp.pad(features, ((0, 0), (32 * q, 96 - 32 * q))) for q in range(4)])
    split1 = lambda w: w.reshape(32, FEATS, 256).transpose(1, 0, 2)
    pad2 = lambda w: jnp.pad(w.reshape(256, FEATS, 1, CLS), ((0, 0), (0, 0), (0, 0), (0, 64 - CLS)))
    w2p = jnp.concatenate([pad2(w_self2), pad2(w_neigh2)], axis=2).reshape(256, 512)
    vm = lambda *shape, dt=F32: pltpu.VMEM(shape, dt)
    dma = pltpu.SemaphoreType.DMA
    whole = pl.BlockSpec(memory_space=pltpu.VMEM)
    loss, gs1, gn1, gs2, gn2 = pl.pallas_call(
        functools.partial(step_kernel, grad_scale),
        out_shape=(
            jax.ShapeDtypeStruct((8, 128), F32),
            jax.ShapeDtypeStruct((32, 1024), F32),
            jax.ShapeDtypeStruct((32, 1024), F32),
            jax.ShapeDtypeStruct((256, 172), F32),
            jax.ShapeDtypeStruct((256, 172), F32),
        ),
        in_specs=[pl.BlockSpec(memory_space=pltpu.SMEM)] + [whole] * 8,
        out_specs=(whole,) * 5,
        scratch_shapes=[
            vm(64, 64, 512, dt=BF), vm(2, 512, 2048, dt=BF), vm(64, 128, 128, dt=BF), vm(36, 128, 128, dt=BF),
            vm(64, 128, 128), vm(64, 128, 128),
            vm(64, 16, 128, dt=BF), vm(64, 16, 128, dt=BF), vm(4, 512, 128, dt=BF),
            vm(4, 32, 256, dt=BF), vm(4, 32, 256, dt=BF), vm(128, 128, dt=BF), vm(4, 128, 128, dt=BF),
            vm(512, 128, dt=BF), vm(512, 128, dt=BF),
            vm(512, 256), vm(512, 256, dt=BF), vm(256, 512, dt=BF), vm(256, 512, dt=BF), vm(4, 512, 128),
            vm(2, 512, 128, dt=BF), vm(4, 256, 128, dt=BF), vm(4, 256, 128), vm(4, 256, 128, dt=BF),
            vm(4, 256, 128), vm(4, 256, 128),
            vm(64, 32, 128, dt=BF), vm(64, 32, 128, dt=BF), vm(4, 8, 512), vm(4, 256, 128, dt=BF),
            vm(64, 32, 128, dt=BF), vm(64, 32, 128, dt=BF), vm(4, 256, 128, dt=BF), vm(512, 512, dt=BF),
            vm(2, 32, 3, 8, 128), vm(32, 3, 8, 128), vm(32, 3, 8, 128), vm(32, 3, 8, 128), vm(3, 8, 128),
            vm(4, 8, 128), vm(32, 2, 8, 128), vm(8, 4, 8, 128), vm(32, 2, 8, 128), vm(8, 4, 8, 128),
            dma, dma, dma((2,)), dma((2,)),
        ] + [dma] * 32,
        compiler_params=pltpu.CompilerParams(
            collective_id=0, has_side_effects=True, vmem_limit_bytes=56 * 1024 * 1024
        ),
    )(
        tile_table(tile_src), xcat, slot_col, slot_row, tile_val.reshape(TILES, 128, 128), labels[:, None],
        split1(w_self1), split1(w_neigh1), w2p,
    )
    return (loss[0, 127] / (ROWS * NODES), gs1, gn1, gs2, gn2)


def solution(mesh):
    in_specs = (
        P("node", "feat"),
        P("node", None, None),
        P("node", None),
        P("node", None),
        P("node", None, None, None),
        P("node"),
        P("feat", None),
        P("feat", None),
        P("feat", None),
        P("feat", None),
    )
    out_specs = (P(), P("feat", None), P("feat", None), P("feat", None), P("feat", None))
    return jax.shard_map(shards, mesh=mesh, in_specs=in_specs, out_specs=out_specs, check_vma=False)
```

time: 572 us -> 142 us (0.25)
  waiting for transfers between devices: 258 us -> 0 us
  blocking collectives: 126 us -> 0 us
  Pallas kernels: 0 us -> 120 us
  local copies, waits for them, and re-layouts: 67.3 us -> 16.1 us
  other arithmetic: 43.3 us -> 2.74 us
  starting transfers between devices: 37.4 us -> 0 us
  matrix products: 23.1 us -> 0 us
  between operations: 15.8 us -> 2.54 us
    psum x1 -> x0, blocking collectives: 126 us -> none  [shards(): mean_loss = lax.psum(jnp.sum(row_loss), 'node') / node_total]
    pallas_call x0 -> x1, Pallas kernels: none -> 120 us  [shards(): pl.pallas_call(functools.partial(step_kernel, grad_scale), out_shape=(jax...]
    all_to_all x3 -> x0, waiting for transfers between devices: 111 us -> none  [the longest x1 50.9 us: shards(): lax.all_to_all(outgoing_two, 'node', split_axis=0, concat_axis=0, tiled=T...]
    psum x2 -> x0, waiting for transfers between devices: 95.9 us -> none  [the longest x1 55.9 us: shards(): summed = lax.psum(local_grads, 'node')]
    all_to_all x3 -> x0, starting transfers between devices: 37.3 us -> none  [the longest x1 13.2 us: shards(): lax.all_to_all(outgoing, 'node', split_axis=0, concat_axis=0, tiled=True)]
    gather x5 -> x0, local copies, waits for them, and re-layouts: 35.3 us -> none  [the longest x3 30.2 us: pack_rows(): picked = jnp.take(own_rows, send_rows[0].reshape(-1), axis=0)]
    reduce_scatter x1 -> x0, waiting for transfers between devices: 29.1 us -> none  [shards(): lax.psum_scatter(partial_one, 'feat', scatter_dimension=1, tiled=True)]
    scatter-add x1 -> x0, other arithmetic: 23.3 us -> none  [shards(): jax.ops.segment_sum(returned.reshape(-1, unit_count), send_rows[0].reshap...]
  transfers between devices with their start and end apart: 7 -> 0, of which waited for: 7 -> 0; matrix products, arithmetic and copies ran while one was open for 1% -> 0% of each run, Pallas kernels for 0% -> 0%
where the time goes in v1:
time: 142 us
  Pallas kernels  120 us (85%)
  local copies, waits for them, and re-layouts  16.1 us (11%)
  other arithmetic  2.74 us (2%)
  between operations  2.54 us (2%)
    pallas_call x1, Pallas kernels, shards(): pl.pallas_call(functools.partial(step_kernel, grad_scale), out_shape=(jax...  120 us
    unnamed x14, local copies, waits for them, and re-layouts  7.57 us

profile of v1, /device:TPU:1, one launch (start us, length us, event | category | flops | bytes accessed | tf_op | source)
XLA Modules:
  0.0 141.5 jit_solution(2978846082253380518)
XLA Ops:
  0.6 0.0 copy-start
  0.6 0.0 copy-start.1
  0.7 0.0 copy-start.3
  0.7 0.0 copy-start.2
  0.7 0.8 reshape.59
  1.5 0.2 convert_reduce_fusion
  1.7 0.2 fusion.5
  1.9 0.1 select_reduce_fusion
  2.0 0.7 concatenate.6.table
  2.7 0.8 copy.43
  3.5 0.7 select_bitcast_fusion
  4.2 0.7 fusion.3
  4.9 0.6 pad.31.slot_col
  5.5 0.1 copy.45
  5.6 0.7 reshape.60.slot_row
  6.3 0.9 reshape.64
  7.2 0.9 reshape.65
  8.2 0.9 copy.50.w2p
  9.0 0.0 copy-done.2
  9.1 0.1 copy.39
  9.2 0.0 copy-done
  9.2 0.0 copy-done.1
  9.2 0.7 bitcast_bitcast_fusion
  9.9 0.0 copy-done.3
  9.9 0.9 copy.49.labels
  10.7 0.2 pad_bitcast_fusion.3
  10.9 0.9 pad_maximum_fusion.xcat
  11.8 120.1 %shard_map.137 = (f32[8,128]{1,0:T(8,128)}, f32[32,1024]{1,0:T(8,128)}, f32[32,1024]{1,0:T(8,128)}, f32[256,172]{1,0:T(8,128)}, f32[256,172]{1,0:T(8,128)}) custom-call(s32[320]{0:T(512)} %concatenate.6.table, bf16[4,512,128]{2,1,0:T(8,128)(2,1)} %pad_maximum_fusion.xcat, s32[64,128]{1,0:T(8,128)} %pad.31.slot_col, s32[2,2048]{1,0:T(2,128)} %reshape.60.slot_row, ...), custom_call_target="tpu_custom_call" | custom-call | tf_op jit(solution)/shard_map/pallas_call | solution.py:484
  131.9 1.3 slice.3
  133.8 1.7 %copy.51 = f32[256,172]{0,1:T(8,128)} copy(f32[256,172]{1,0:T(8,128)} %get-tuple-element.28) | data formatting | bytes 352256
  135.5 1.7 %copy.52 = f32[256,172]{0,1:T(8,128)} copy(f32[256,172]{1,0:T(8,128)} %get-tuple-element.29) | data formatting | bytes 352256
  137.3 1.6 %copy.59 = f32[32,1024]{1,0:T(8,128)} copy(f32[32,1024]{1,0:T(8,128)} %get-tuple-element.48) | data formatting | bytes 262144
  138.8 1.6 %copy.60 = f32[32,1024]{1,0:T(8,128)} copy(f32[32,1024]{1,0:T(8,128)} %get-tuple-element.49) | data formatting | bytes 262144
  (6 shorter events, 0.1 us)
Async XLA Ops:
  0.6 8.5 %copy-start = (bf16[32,1024]{1,0:T(8,128)(2,1)S(1)}, bf16[32,1024]{1,0:T(8,128)(2,1)}, u32[]{:S(2)}) copy-start(bf16[32,1024]{1,0:T(8,128)(2,1)} %param.17) | copy-start | bytes 196612
  0.6 8.5 %copy-start.1 = (bf16[32,1024]{1,0:T(8,128)(2,1)S(1)}, bf16[32,1024]{1,0:T(8,128)(2,1)}, u32[]{:S(2)}) copy-start(bf16[32,1024]{1,0:T(8,128)(2,1)} %param.16) | copy-start | bytes 196612
  0.7 9.2 %copy-start.3 = (s32[512]{0:T(512)S(1)}, s32[512]{0:T(512)}, u32[]{:S(2)}) copy-start(s32[512]{0:T(512)} %param.15) | copy-start | bytes 6148
  0.7 8.4 %copy-start.2 = (bf16[512,32]{0,1:T(8,128)(2,1)S(1)}, bf16[512,32]{0,1:T(8,128)(2,1)}, u32[]{:S(2)}) copy-start(bf16[512,32]{0,1:T(8,128)(2,1)} %param.10) | copy-start | bytes 98308

commit v2 on v0

v2 whole, which is shorter than its diff:
```python
import functools
import math

import jax
import jax.numpy as jnp
from jax import lax
from jax.experimental import pallas as pl
from jax.experimental.pallas import tpu as pltpu
from jax.sharding import PartitionSpec as P

MESH = pl.DeviceIdType.MESH
F32 = jnp.float32
BF = jnp.bfloat16
I32 = jnp.int32
ROWS = 512
SLOTS = 64
NODES = 64
FEATS = 4
CHIPS = NODES // 2
RINGS = 4
TILES = 64
CLASSES = 172
CLS = 43
TALL = 176
CLS_TILES = TALL // 8
GELU_C = math.sqrt(2.0 / math.pi)


def lane_roll(value, shift):
    shift = shift % value.shape[-1]
    return pltpu.roll(value, shift, value.ndim - 1) if shift else value


def dot(a, b):
    return jnp.dot(a, b, preferred_element_type=F32)


def dot_nt(a, b):
    return lax.dot_general(a, b, (((1,), (1,)), ((), ())), preferred_element_type=F32)


def iota(shape, axis):
    return lax.broadcasted_iota(I32, shape, axis)


def g1_row(chip):
    y, z = chip // 8, chip % 8
    keep = (y + z) % 4
    rt = y * 2 + z // 4
    return (rt // 4) * 128 + 32 * keep + 8 * (rt % 4)


def step_kernel(
    grad_scale,
    tile_src, feat_t, send_rows, send_count, tiles_hbm, labels, w1s, w1n, w2s_t, w2n_t,
    fin_a, half_a, fin_b, half_b, fin_c, half_c,
    tiles, xcat, slot_col, wide, w2p_t, order_v, order,
    hot, hot_t, tiles_t, src, run, ptile,
    out1, recv1, xrecv, w1s_full, w1n_full, aggp, agg_recv, xfull, aggf,
    slope, hid, xa_t, pf, ycat, ypack, yown, yrecv, spack, srecv,
    out2, recv2, stat, dlp, ret, recvb, gp, dlcat, dlcat_t, gcat,
    da, pa, db, pb, dc, pc, ra, rb, rc, ta, tb, tc, trecv,
    s_tiles, s_order, s_x, r_x, s_w, r_w, s_e1, r_e1, s_agg, r_agg, s_y, r_y, s_s, r_s, s_e2, r_e2,
    s_st, r_st, s_dl, r_dl, s_eb, r_eb, s_g, r_g, s_pair, r_pair, s_red, r_red,
    s_t, r_t, s_fin, r_fin, s_half, r_half,
):
    me = lax.axis_index("node")
    f = lax.axis_index("feat")
    chip, core = me // 2, lax.rem(me, 2)
    ring, place = me // 16, lax.rem(me // 2, 8)
    partner = me + 1 - 2 * core

    def wait_bytes(ref, sem):
        pltpu.make_async_copy(ref, ref, sem).wait()

    def send(s, d, ssem, rsem, node, feat):
        pltpu.make_async_remote_copy(
            src_ref=s, dst_ref=d, send_sem=ssem, recv_sem=rsem,
            device_id=(node, feat), device_id_type=MESH,
        ).start()

    def to_feats(s, d, ssem, rsem, same=False):
        for i in (2, 1, 3):
            g = lax.rem(f + i, FEATS)
            send(s if same else s.at[g], d.at[f], ssem, rsem, me, g)

    def place_at(k):
        off = ((k + 1) // 2) * (2 * lax.rem(k, 2) - 1)
        return lax.rem(place + off + 8, 8)

    def ring_at(j):
        return lax.rem(ring + (2, 1, 3, 0)[j], RINGS)

    lane = lambda r, n=128: iota((r, n), 1)
    three = pl.ds(0, FEATS - 1)

    load_tiles = pltpu.make_async_copy(tiles_hbm, tiles, s_tiles)
    load_tiles.start()

    bar = pltpu.get_barrier_semaphore()

    def hello(i, c):
        pl.semaphore_signal(bar, inc=1, device_id=(lax.rem(me + i, NODES), f), device_id_type=MESH)
        return c

    lax.fori_loop(1, NODES, hello, 0)
    for i in range(1, FEATS):
        pl.semaphore_signal(bar, inc=1, device_id=(me, lax.rem(f + i, FEATS)), device_id_type=MESH)

    x0 = jnp.transpose(jnp.concatenate([feat_t[...].astype(F32), jnp.zeros((96, ROWS), F32)], axis=0))
    for q in range(4):
        xcat[q] = lane_roll(x0, 32 * q).astype(BF)

    wide[0, 0:64, 0:64] = send_rows[...].astype(F32)
    turned = jnp.transpose(wide[0, 0:128, 0:128]).astype(I32)[0:64]
    counts = jnp.concatenate([send_count[...], jnp.zeros((1, 64), I32)], axis=1)
    slot_col[...] = jnp.where(iota((64, 128), 0) < counts, turned, -1)

    def build_hot(d, c):
        col = jnp.sum(jnp.where(lane(SLOTS) == d, slot_col[...], 0), axis=1, keepdims=True)
        hot[d] = jnp.where(col == lane(SLOTS, ROWS), 1.0, 0.0).astype(BF)
        return c

    lax.fori_loop(0, NODES, build_hot, 0, unroll=8)
    pl.semaphore_wait(bar, NODES - 1 + FEATS - 1)

    for j in range(RINGS):
        rr = ring_at(j)
        d0 = pl.multiple_of(rr * 16, 16)
        acc = jnp.zeros((256, 128), F32)
        for q in range(4):
            acc = acc + dot(hot[pl.ds(d0, 16), 16 * q:16 * q + 16, :].reshape(256, ROWS), xcat[q])
        out1[pl.ds(d0, 16)] = acc.astype(BF).reshape(16, 16, 128)

        def send1(k, c):
            k = (16 if j < 3 else 15) - 1 - k + (0 if j < 3 else 1)
            p = rr * 16 + place_at(k // 2) * 2 + lax.rem(core + k, 2)
            send(out1.at[p], recv1.at[me], s_e1, r_e1.at[ring], p, f)
            return c

        lax.fori_loop(0, 16 if j < 3 else 15, send1, 0)
    for i in (2, 1, 3):
        g = lax.rem(f + i, FEATS)
        cols = pl.ds(pl.multiple_of(g * 256, 256), 256)
        send(xcat.at[f], xrecv.at[f], s_x, r_x, me, g)
        send(w1s.at[:, cols], w1s_full.at[f], s_w.at[0], r_w.at[0], me, g)
        send(w1n.at[:, cols], w1n_full.at[f], s_w.at[1], r_w.at[1], me, g)

    recv1[me] = out1[me]
    xrecv[f] = xcat[f]
    own_cols = pl.ds(pl.multiple_of(f * 256, 256), 256)
    w1s_full[f] = w1s[:, own_cols]
    w1n_full[f] = w1n[:, own_cols]
    for b in range(4):
        src[b] = xcat[0, 128 * b:128 * b + 128, :]

    for part, ref in enumerate((w2s_t, w2n_t)):
        wide[0, 0:CLASSES, 0:256] = ref[...].astype(F32)
        wide[1] = jnp.zeros((256, 256), F32)
        for g in range(4):
            wide[1, 64 * g:64 * g + CLS, :] = wide[0, CLS * g:CLS * g + CLS, 0:256]
        w2p_t[256 * part:256 * part + 256, :] = wide[1].astype(BF)

    srow = jnp.full((128, 128), 1 << 20, I32)
    for t in range(TILES):
        srow = jnp.where(lane(128) == t, tile_src[t // 16, t % 16], srow)
    scol = jnp.transpose(srow)
    sub = iota((128, 128), 0)
    lane128 = lane(128)
    same = (srow == scol) & (lane128 < sub)
    rank = jnp.sum(jnp.where((srow < scol) | same, 1, 0), axis=1, keepdims=True)
    goes = jnp.minimum(jnp.sum(jnp.where(same, 1, 0), axis=1, keepdims=True), 1)
    at = rank == lane128
    order_v[...] = jnp.zeros((8, 128), I32)
    order_v[0:1, :] = jnp.sum(jnp.where(at, sub, 0), axis=0, keepdims=True)
    order_v[1:2, :] = jnp.sum(jnp.where(at, goes, 0), axis=0, keepdims=True)
    upto = jnp.sum(jnp.where(scol <= lane128, 1, 0), axis=0, keepdims=True)
    order_v[2:3, :] = jnp.maximum(upto - 1, 0)
    order_v[3:4, :] = jnp.minimum(jnp.sum(jnp.where(scol == lane128, 1, 0), axis=0, keepdims=True), 1)
    order_copy = pltpu.make_async_copy(order_v, order, s_order)
    order_copy.start()

    load_tiles.wait()

    def turn(t, c):
        tiles_t[t] = jnp.transpose(tiles[t])
        return c

    lax.fori_loop(0, TILES, turn, 0, unroll=4)
    order_copy.wait()

    def row_bytes(buf, j):
        return buf.at[pl.ds(0, 15 if j == 3 else 16)]

    for j in (3, 1, 2, 0):
        rr = ring_at(j)
        wait_bytes(row_bytes(recv1, j), r_e1.at[rr])

        def unpack1(k, c):
            b = rr * 8 + k
            for p in range(2):
                v = recv1[2 * b + p].astype(F32)
                for q in range(4):
                    src[4 + b, 64 * p + 16 * q:64 * p + 16 * q + 16, :] = lane_roll(v, -32 * q).astype(BF)
            return c

        lax.fori_loop(0, 8, unpack1, 0, unroll=4)

    def tile_product(b):
        lhs = jnp.concatenate([tiles[16 * b + k] for k in range(16)], axis=1)
        rhs = jnp.concatenate([src[tile_src[b, k]] for k in range(16)], axis=0)
        return dot(lhs, rhs)

    packed = jnp.zeros((128, 128), F32)
    group = lane128 // 32
    for b in range(4):
        packed = packed + lane_roll(jnp.where(group == 0, tile_product(b), 0.0), 32 * b)
    aggp[...] = packed.astype(BF)
    to_feats(aggp, agg_recv, s_agg, r_agg, same=True)
    agg_recv[f] = aggp[...]

    wait_bytes(xrecv.at[three], r_x)
    wait_bytes(w1s_full.at[three], r_w.at[0])
    wait_bytes(w1n_full.at[three], r_w.at[1])
    xfull[...] = xrecv[0] + xrecv[1] + xrecv[2] + xrecv[3]
    pre0 = dot(xfull[...], w1s_full[...].reshape(128, 256))
    wait_bytes(agg_recv.at[three], r_agg)
    for b in range(4):
        acc = jnp.zeros((128, 128), F32)
        for g in range(4):
            acc = jnp.where(group == g, lane_roll(agg_recv[g].astype(F32), 32 * (g - b)), acc)
        aggf[128 * b:128 * b + 128, :] = acc.astype(BF)

    pre = pre0 + dot(aggf[...], w1n_full[...].reshape(128, 256))
    th = jnp.tanh(GELU_C * (pre + 0.044715 * (pre * pre * pre)))
    cdf = 0.5 * (1.0 + th)
    slope[...] = cdf + pre * (0.5 * (1.0 - th * th)) * (GELU_C * (1.0 + 3.0 * 0.044715 * (pre * pre)))
    hid[...] = (pre * cdf).astype(BF)

    low256 = lane(256) < 64

    def pack_halves(v, g):
        a, b = v[0:256], v[256:512]
        return jnp.where(low256, a if g % 2 == 0 else lane_roll(a, 64), lane_roll(b, 64) if g % 2 == 0 else b)

    for half in range(2):
        v = dot_nt(hid[...], w2p_t[256 + 128 * half:256 + 128 * half + 128, :])
        for g in (2 * half, 2 * half + 1):
            yv = pack_halves(v, g)
            yown[g] = yv
            ypack[g] = yv.astype(BF)
    to_feats(ypack, yrecv, s_y, r_y)
    for half in range(2):
        v = dot_nt(hid[...], w2p_t[128 * half:128 * half + 128, :])
        for g in (2 * half, 2 * half + 1):
            spack[g] = pack_halves(v, g)
    to_feats(spack, srecv, s_s, r_s)
    yrecv[f] = jnp.zeros((256, 128), BF)
    srecv[f] = spack[f]
    wait_bytes(yrecv.at[three], r_y)
    ys = yown[f]
    for g in range(4):
        ys = ys + yrecv[g].astype(F32)
    yr = lane_roll(ys, 64)
    ycat[0, 0:256, :] = jnp.where(low256, ys, 0.0).astype(BF)
    ycat[0, 256:512, :] = jnp.where(low256, yr, 0.0).astype(BF)
    ycat[1, 0:256, :] = jnp.where(low256, 0.0, yr).astype(BF)
    ycat[1, 256:512, :] = jnp.where(low256, 0.0, ys).astype(BF)

    for j in range(RINGS):
        rr = ring_at(j)
        d0 = pl.multiple_of(rr * 16, 16)
        acc = dot(hot[pl.ds(d0, 16), 0:32, :].reshape(512, ROWS), ycat[0])
        acc = acc + dot(hot[pl.ds(d0, 16), 32:64, :].reshape(512, ROWS), ycat[1])
        out2[pl.ds(d0, 16)] = acc.astype(BF).reshape(16, 32, 128)

        def send2(k, c):
            k = (16 if j < 3 else 15) - 1 - k + (0 if j < 3 else 1)
            p = rr * 16 + place_at(k // 2) * 2 + lax.rem(core + k, 2)
            send(out2.at[p], recv2.at[me], s_e2, r_e2.at[ring], p, f)
            return c

        lax.fori_loop(0, 16 if j < 3 else 15, send2, 0)

    recv2[me] = out2[me]
    for b in range(4):
        src[b] = ycat[0, 128 * b:128 * b + 128, :]
    xa_t[0:128, :] = jnp.transpose(xfull[...])
    xa_t[128:256, :] = jnp.transpose(aggf[...])

    def turn_hot(y, c):
        d0 = pl.multiple_of(y * 16, 16)
        for h in range(2):
            for k in range(4):
                part = hot[pl.ds(d0, 16), 32 * h:32 * h + 32, 128 * k:128 * k + 128].reshape(512, 128)
                hot_t[y, h, 128 * k:128 * k + 128, :] = jnp.transpose(part)
        return c

    lax.fori_loop(0, RINGS, turn_hot, 0)

    for j in (3, 1, 2, 0):
        rr = ring_at(j)
        wait_bytes(row_bytes(recv2, j), r_e2.at[rr])

        def unpack2(k, c):
            b = rr * 8 + k
            for p in range(2):
                v = recv2[2 * b + p]
                src[4 + b, 64 * p:64 * p + 32, :] = v
                src[4 + b, 64 * p + 32:64 * p + 64, :] = lane_roll(v.astype(F32), 64).astype(BF)
            return c

        lax.fori_loop(0, 8, unpack2, 0, unroll=4)

    wait_bytes(srecv.at[three], r_s)
    ss = srecv[0] + srecv[1] + srecv[2] + srecv[3]
    pf[0, 0:256, :] = ss
    pf[0, 256:512, :] = lane_roll(ss, 64)

    mine = lane128 < CLS
    for b in range(4):
        r = slice(128 * b, 128 * b + 128)
        lg = jnp.where(mine, pf[0, r, :] + tile_product(b), -1e30)
        top = jnp.max(lg, axis=1, keepdims=True)
        ex = jnp.exp(lg - top)
        tot = jnp.sum(ex, axis=1, keepdims=True)
        lab = jnp.transpose(jnp.broadcast_to(labels[b:b + 1, :].astype(F32), (128, 128))).astype(I32)
        want = mine & ((lab - CLS * f) == lane128)
        hit = jnp.sum(jnp.where(want, lg, 0.0), axis=1, keepdims=True)
        st = jnp.where(lane128 == 0, top, jnp.where(lane128 == 1, tot, jnp.where(lane128 == 2, hit, 0.0)))
        stat[f, :, r] = jnp.transpose(st)[0:8, :]
        pf[1, r, :] = ex
        pf[2, r, :] = jnp.where(want, 1.0, 0.0)
    to_feats(stat.at[f], stat, s_st, r_st, same=True)
    wait_bytes(stat.at[three], r_st)

    tops = [stat[g, 0:1, :] for g in range(4)]
    best = jnp.maximum(jnp.maximum(tops[0], tops[1]), jnp.maximum(tops[2], tops[3]))
    total = jnp.zeros_like(best)
    hits = jnp.zeros_like(best)
    for g in range(4):
        total = total + stat[g, 1:2, :] * jnp.exp(tops[g] - best)
        hits = hits + stat[g, 2:3, :]
    loss = jnp.sum(jnp.log(total) + best - hits)
    factor = jnp.broadcast_to(jnp.exp(stat[f, 0:1, :] - best) / total, (128, ROWS))
    for b in range(4):
        r = slice(128 * b, 128 * b + 128)
        fac = jnp.transpose(factor[:, 128 * b:128 * b + 128])
        dl = ((pf[1, r, :] * fac - pf[2, r, :]) * grad_scale).astype(BF)
        rows = slice(128 * (b % 2), 128 * (b % 2) + 128)
        if b < 2:
            dlp[f, rows, :] = dl
        else:
            dlp[f, rows, :] = (dlp[f, rows, :].astype(F32) + lane_roll(dl.astype(F32), 64)).astype(BF)
        lhs = tiles_t[16 * b:16 * b + 16].reshape(2048, 128)
        ptile[16 * b:16 * b + 16] = dot(lhs, dl).reshape(16, 128, 128)
    to_feats(dlp.at[f], dlp, s_dl, r_dl, same=True)

    def gather_sum(t, acc):
        acc = acc * order[1, t].astype(F32) + ptile[order[0, t]]
        run[t] = acc
        return acc

    lax.fori_loop(0, TILES, gather_sum, jnp.zeros((128, 128), F32), unroll=4)

    def landed(j):
        return run[order[2, j]] * order[3, j].astype(F32)

    for j in range(RINGS):
        rr = ring_at(j)

        def pack_back(k, c):
            to = rr * 8 + place_at(7 - k)
            blk = landed(4 + to)
            for p in range(2):
                v = blk[64 * p:64 * p + 32, :] + lane_roll(blk[64 * p + 32:64 * p + 64, :], 64)
                ret[2 * to + p] = v.astype(BF)
            return c

        lax.fori_loop(0, 8, pack_back, 0, unroll=4)

        def send_back(k, c):
            k = (16 if j < 3 else 15) - 1 - k + (0 if j < 3 else 1)
            p = rr * 16 + place_at(k // 2) * 2 + lax.rem(core + k, 2)
            send(ret.at[p], recvb.at[me], s_eb, r_eb.at[ring], p, f)
            return c

        lax.fori_loop(0, 16 if j < 3 else 15, send_back, 0)

    recvb[me] = ret[me]
    for b in range(4):
        pf[3, 128 * b:128 * b + 128, :] = landed(b)

    def join(ref, out):
        for pair in range(2):
            c = slice(128 * pair, 128 * pair + 128)
            a, b = ref[2 * pair].astype(F32), ref[2 * pair + 1].astype(F32)
            out[0:256, c] = jnp.where(low256, a, lane_roll(b, 64)).astype(BF)
            out[256:512, c] = jnp.where(low256, lane_roll(a, 64), b).astype(BF)

    def class_rows(v, d):
        for l in range(2):
            d[l, TALL - 8:TALL, :] = jnp.zeros((8, 128), F32)
            for g in range(4):
                d[l, CLS * g:CLS * g + CLS, :] = v[64 * g:64 * g + CLS, 128 * l:128 * l + 128]

    def rows8(t):
        return pl.ds(pl.multiple_of(t * 8, 8), 8)

    def chip_at(i):
        return lax.rem(ring + (i // 8) + 4, RINGS) * 8 + place_at(lax.rem(i, 8))

    def for_chips(body):
        lax.fori_loop(1, CHIPS, lambda i, c: (body(chip_at(CHIPS - i)), c)[1], 0)

    def reduce_class(d, peer, part, k):
        wait_bytes(peer, r_pair.at[k])
        d[core] = d[core] + peer[...]

        def one(p):
            @pl.when(p < CLS_TILES)
            def _():
                send(d.at[core, rows8(p)], part.at[chip], s_red.at[k], r_red.at[k], 2 * p + core, f)

        for_chips(one)

        @pl.when(chip < CLS_TILES)
        def _():
            part[chip] = d[core, rows8(chip), :]

    def spread_class(part, tile, fin, k):
        @pl.when(chip < CLS_TILES)
        def _():
            wait_bytes(part.at[pl.ds(0, CHIPS - 1)], r_red.at[k])
            tile[...] = jnp.sum(part[...], axis=0)
            for_chips(lambda p: send(tile, fin.at[chip], s_fin.at[k], r_fin.at[k], 2 * p + core, f))
            fin[chip] = tile[...]

    def gather_class(fin, half, k):
        @pl.when(chip < CLS_TILES)
        def _():
            wait_bytes(fin.at[pl.ds(0, CLS_TILES - 1)], r_fin.at[k])

        @pl.when(chip >= CLS_TILES)
        def _():
            wait_bytes(fin, r_fin.at[k])

        send(fin, half, s_half.at[k], r_half.at[k], partner, f)

    wait_bytes(dlp.at[three], r_dl)
    join(dlp, dlcat)
    dlcat_t[...] = jnp.transpose(dlcat[...])
    class_rows(dot(dlcat_t[...], hid[...]), da)
    tail = (iota((8, 128), 0) == 7) & (lane(8) == 0)
    for l in range(2):
        da[l, TALL - 8:TALL, :] = da[l, TALL - 8:TALL, :] + jnp.where(tail, loss, 0.0)
    send(da.at[1 - core], pa, s_pair.at[0], r_pair.at[0], partner, f)
    reduce_class(da, pa, ra, 0)

    g_sum = pf[3]
    low = lane(ROWS) < 64
    for j in (3, 1, 2, 0):
        rr = ring_at(j)
        wait_bytes(row_bytes(recvb, j), r_eb.at[rr])
        back = recvb[pl.ds(pl.multiple_of(rr * 16, 16), 16)].reshape(512, 128)
        g_sum = g_sum + jnp.where(low, dot(hot_t[rr, 0], back), 0.0)
        g_sum = g_sum + jnp.where(low, lane_roll(dot(hot_t[rr, 1], back), 64), 0.0)
    gp[f] = (g_sum[0:256] + lane_roll(g_sum[256:512], 64)).astype(BF)
    to_feats(gp.at[f], gp, s_g, r_g, same=True)
    spread_class(ra, ta, fin_a, 0)
    bh0 = dot(dlcat[...], w2p_t[0:256, :])
    wait_bytes(gp.at[three], r_g)
    join(gp, gcat)

    class_rows(dot(jnp.transpose(gcat[...]), hid[...]), db)
    send(db.at[1 - core], pb, s_pair.at[1], r_pair.at[1], partner, f)
    bh = bh0 + dot(gcat[...], w2p_t[256:512, :])
    g1 = dot(xa_t[...], (bh * slope[...]).astype(BF))
    for l in range(2):
        for ch in range(CHIPS):
            dc[l, ch] = g1[g1_row(ch):g1_row(ch) + 8, 128 * l:128 * l + 128]
    send(dc.at[1 - core], pc, s_pair.at[2], r_pair.at[2], partner, f)
    wait_bytes(pc, r_pair.at[2])
    dc[core] = dc[core] + pc[...]
    for_chips(lambda p: send(dc.at[core, p], rc.at[chip], s_red.at[2], r_red.at[2], 2 * p + core, f))
    rc[chip] = dc[core, chip]
    reduce_class(db, pb, rb, 1)

    wait_bytes(rc.at[pl.ds(0, CHIPS - 1)], r_red.at[2])
    tc[...] = jnp.sum(rc[...], axis=0)
    keep = lax.rem(ring + place, 4)
    rt = ring * 2 + place // 4
    kept = keep == f

    @pl.when(jnp.logical_not(kept))
    def _():
        send(tc, trecv.at[f], s_t, r_t, me, keep)

    spread_class(rb, tb, fin_b, 1)

    @pl.when(kept)
    def _():
        trecv[f] = tc[...]
        wait_bytes(trecv.at[three], r_t)
        for_chips(lambda p: send(trecv, fin_c.at[rt], s_fin.at[2], r_fin.at[2], 2 * p + core, f))
        fin_c[rt] = trecv[...]

    gather_class(fin_a, half_a, 0)
    gather_class(fin_b, half_b, 1)

    @pl.when(kept)
    def _():
        wait_bytes(fin_c.at[pl.ds(0, 7)], r_fin.at[2])

    @pl.when(jnp.logical_not(kept))
    def _():
        wait_bytes(fin_c, r_fin.at[2])

    send(fin_c, half_c, s_half.at[2], r_half.at[2], partner, f)

    n63, c31 = pl.ds(0, NODES - 1), pl.ds(0, CHIPS - 1)
    wait_bytes(recv1.at[n63], s_e1)
    wait_bytes(xrecv.at[three], s_x)
    wait_bytes(w1s_full.at[three], s_w.at[0])
    wait_bytes(w1n_full.at[three], s_w.at[1])
    wait_bytes(agg_recv.at[three], s_agg)
    wait_bytes(yrecv.at[three], s_y)
    wait_bytes(srecv.at[three], s_s)
    wait_bytes(recv2.at[n63], s_e2)
    wait_bytes(stat.at[three], s_st)
    wait_bytes(dlp.at[three], s_dl)
    wait_bytes(recvb.at[n63], s_eb)
    wait_bytes(gp.at[three], s_g)
    wait_bytes(pa, s_pair.at[0])
    wait_bytes(pb, s_pair.at[1])
    wait_bytes(pc, s_pair.at[2])
    wait_bytes(rc.at[c31], s_red.at[2])
    for k, part in ((0, ra), (1, rb)):
        @pl.when(chip < CLS_TILES)
        def _():
            wait_bytes(part.at[pl.ds(0, CLS_TILES - 1)], s_red.at[k])
            wait_bytes(part.at[c31], s_fin.at[k])

        @pl.when(chip >= CLS_TILES)
        def _():
            wait_bytes(part.at[pl.ds(0, CLS_TILES)], s_red.at[k])

    @pl.when(jnp.logical_not(kept))
    def _():
        wait_bytes(trecv.at[0], s_t)

    @pl.when(kept)
    def _():
        wait_bytes(ptile.at[c31, pl.ds(0, 32)], s_fin.at[2])

    for k, ref in enumerate((half_a, half_b, half_c)):
        wait_bytes(ref, s_half.at[k])
        wait_bytes(ref, r_half.at[k])


def result_kernel(scale, fin_a, half_a, fin_b, half_b, fin_c, half_c, loss_ref, gs1_ref, gn1_ref, gs2_ref, gn2_ref):
    core = lax.rem(lax.axis_index("node"), 2)
    first = core == 0
    loss_ref[...] = fin_a[CLS_TILES - 1, 7:8, 0:1] * scale
    for l in range(2):
        c = slice(128 * l, 128 * l + 128)
        mine = first if l == 0 else jnp.logical_not(first)
        for fin, half, ref in ((fin_a, half_a, gs2_ref), (fin_b, half_b, gn2_ref)):
            ref[:, c] = jnp.where(mine, fin[...], half[...]).reshape(TALL, 128)[0:CLASSES]
        v = jnp.where(mine, fin_c[...], half_c[...])
        for g in range(4):
            cols = slice(256 * g + 128 * l, 256 * g + 128 * l + 128)
            gs1_ref[:, cols] = v[0:4, g].reshape(32, 128)
            gn1_ref[:, cols] = v[4:8, g].reshape(32, 128)


def shards(features, send_rows, send_count, tile_src, tile_val, labels, w_self1, w_neigh1, w_self2, w_neigh2):
    vm = lambda *shape, dt=F32: pltpu.VMEM(shape, dt)
    dma = pltpu.SemaphoreType.DMA
    whole = pl.BlockSpec(memory_space=pltpu.VMEM)
    half_class = jax.ShapeDtypeStruct((CLS_TILES, 8, 128), F32)
    half_first = jax.ShapeDtypeStruct((8, 4, 8, 128), F32)
    parts = pl.pallas_call(
        functools.partial(step_kernel, 1.0 / math.sqrt(ROWS * NODES)),
        out_shape=(half_class,) * 4 + (half_first,) * 2,
        in_specs=[pl.BlockSpec(memory_space=pltpu.SMEM)] + [whole] * 3 + [pl.BlockSpec(memory_space=pl.ANY)] + [whole] * 5,
        out_specs=(whole,) * 6,
        scratch_shapes=[
            vm(64, 128, 128, dt=BF), vm(4, 512, 128, dt=BF), vm(64, 128, dt=I32), vm(2, 256, 256),
            vm(512, 256, dt=BF), vm(8, 128, dt=I32), pltpu.SMEM((8, 128), I32),
            vm(64, 64, 512, dt=BF), vm(4, 2, 512, 512, dt=BF), vm(64, 128, 128, dt=BF), vm(36, 128, 128, dt=BF),
            vm(64, 128, 128), vm(64, 128, 128),
            vm(64, 16, 128, dt=BF), vm(64, 16, 128, dt=BF), vm(4, 512, 128, dt=BF),
            vm(4, 32, 256, dt=BF), vm(4, 32, 256, dt=BF), vm(128, 128, dt=BF), vm(4, 128, 128, dt=BF),
            vm(512, 128, dt=BF), vm(512, 128, dt=BF),
            vm(512, 256), vm(512, 256, dt=BF), vm(256, 512, dt=BF), vm(4, 512, 128),
            vm(2, 512, 128, dt=BF), vm(4, 256, 128, dt=BF), vm(4, 256, 128), vm(4, 256, 128, dt=BF),
            vm(4, 256, 128), vm(4, 256, 128),
            vm(64, 32, 128, dt=BF), vm(64, 32, 128, dt=BF), vm(4, 8, 512), vm(4, 256, 128, dt=BF),
            vm(64, 32, 128, dt=BF), vm(64, 32, 128, dt=BF), vm(4, 256, 128, dt=BF),
            vm(512, 256, dt=BF), vm(256, 512, dt=BF), vm(512, 256, dt=BF),
            vm(2, TALL, 128), vm(TALL, 128), vm(2, TALL, 128), vm(TALL, 128), vm(2, 32, 8, 128), vm(32, 8, 128),
            vm(32, 8, 128), vm(32, 8, 128), vm(32, 8, 128), vm(8, 128), vm(8, 128), vm(8, 128), vm(4, 8, 128),
            dma, dma, dma, dma, dma((2,)), dma((2,)), dma, dma((4,)), dma, dma, dma, dma, dma, dma, dma, dma((4,)),
            dma, dma, dma, dma, dma, dma((4,)), dma, dma, dma((3,)), dma((3,)), dma((3,)), dma((3,)),
            dma, dma, dma((3,)), dma((3,)), dma((3,)), dma((3,)),
        ],
        compiler_params=pltpu.CompilerParams(
            collective_id=0, has_side_effects=True, vmem_limit_bytes=56 * 1024 * 1024
        ),
    )(
        tile_src, features.T, send_rows[0], send_count, tile_val.reshape(TILES, 128, 128), labels.reshape(4, 128),
        w_self1, w_neigh1, w_self2.T, w_neigh2.T,
    )
    loss, gs1, gn1, gs2, gn2 = pl.pallas_call(
        functools.partial(result_kernel, 1.0 / (ROWS * NODES)),
        out_shape=(
            jax.ShapeDtypeStruct((1, 1), F32),
            jax.ShapeDtypeStruct((32, 1024), F32),
            jax.ShapeDtypeStruct((32, 1024), F32),
            jax.ShapeDtypeStruct((CLASSES, 256), F32),
            jax.ShapeDtypeStruct((CLASSES, 256), F32),
        ),
        in_specs=[whole] * 6,
        out_specs=(whole,) * 5,
    )(*parts)
    return (loss[0, 0], gs1, gn1, gs2.T, gn2.T)


def solution(mesh):
    in_specs = (
        P("node", "feat"),
        P("node", None, None),
        P("node", None),
        P("node", None),
        P("node", None, None, None),
        P("node"),
        P("feat", None),
        P("feat", None),
        P("feat", None),
        P("feat", None),
    )
    out_specs = (P(), P("feat", None), P("feat", None), P("feat", None), P("feat", None))
    return jax.shard_map(shards, mesh=mesh, in_specs=in_specs, out_specs=out_specs, check_vma=False)
```

time: 572 us -> 104 us (0.18)
  waiting for transfers between devices: 258 us -> 0 us
  blocking collectives: 126 us -> 0 us
  Pallas kernels: 0 us -> 104 us
  local copies, waits for them, and re-layouts: 67.3 us -> 0 us
  other arithmetic: 43.3 us -> 0 us
  starting transfers between devices: 37.4 us -> 0 us
  matrix products: 23.1 us -> 0 us
  between operations: 15.8 us -> 0.64 us
    psum x1 -> x0, blocking collectives: 126 us -> none  [shards(): mean_loss = lax.psum(jnp.sum(row_loss), 'node') / node_total]
    all_to_all x3 -> x0, waiting for transfers between devices: 111 us -> none  [the longest x1 50.9 us: shards(): lax.all_to_all(outgoing_two, 'node', split_axis=0, concat_axis=0, tiled=T...]
    pallas_call x0 -> x2, Pallas kernels: none -> 104 us  [the longest x1 102 us: shards(): pl.pallas_call(functools.partial(step_kernel, 1.0 / math.sqrt(ROWS * NODE...]
    psum x2 -> x0, waiting for transfers between devices: 95.9 us -> none  [the longest x1 55.9 us: shards(): summed = lax.psum(local_grads, 'node')]
    all_to_all x3 -> x0, starting transfers between devices: 37.3 us -> none  [the longest x1 13.2 us: shards(): lax.all_to_all(outgoing, 'node', split_axis=0, concat_axis=0, tiled=True)]
    gather x5 -> x0, local copies, waits for them, and re-layouts: 35.3 us -> none  [the longest x3 30.2 us: pack_rows(): picked = jnp.take(own_rows, send_rows[0].reshape(-1), axis=0)]
    reduce_scatter x1 -> x0, waiting for transfers between devices: 29.1 us -> none  [shards(): lax.psum_scatter(partial_one, 'feat', scatter_dimension=1, tiled=True)]
    scatter-add x1 -> x0, other arithmetic: 23.3 us -> none  [shards(): jax.ops.segment_sum(returned.reshape(-1, unit_count), send_rows[0].reshap...]
  transfers between devices with their start and end apart: 7 -> 0, of which waited for: 7 -> 0; matrix products, arithmetic and copies ran while one was open for 1% -> 0% of each run, Pallas kernels for 0% -> 0%
where the time goes in v2:
time: 104 us
  Pallas kernels  104 us (100%)
    pallas_call x1, Pallas kernels, shards(): pl.pallas_call(functools.partial(step_kernel, 1.0 / math.sqrt(ROWS * NODE...  102 us

profile of v2, /device:TPU:1, one launch (start us, length us, event | category | flops | bytes accessed | tf_op | source)
XLA Modules:
  0.0 104.3 jit_solution(84356534922467151)
XLA Ops:
  0.6 101.6 %shard_map.137 = (f32[22,8,128]{2,1,0:T(8,128)}, f32[22,8,128]{2,1,0:T(8,128)}, f32[22,8,128]{2,1,0:T(8,128)}, f32[22,8,128]{2,1,0:T(8,128)}, f32[8,4,8,128]{3,2,1,0:T(8,128)}, /*index=5*/f32[8,4,8,128]{3,2,1,0:T(8,128)}) custom-call(s32[4,16]{1,0:T(4,128)} %tile_src.1, bf16[32,512]{1,0:T(8,128)(2,1)} %bitcast.12, s32[64,64]{1,0:T(8,128)} %bitcast.13, ...), custom_call_target="tpu_custom_call" | custom-call | tf_op jit(solution)/shard_map/pallas_call | solution.py:583
  102.3 2.0 %shard_map.138 = (f32[1,1]{1,0:T(1,128)}, f32[32,1024]{1,0:T(8,128)}, f32[32,1024]{1,0:T(8,128)}, f32[172,256]{1,0:T(8,128)}, f32[172,256]{1,0:T(8,128)}) custom-call(f32[22,8,128]{2,1,0:T(8,128)} %get-tuple-element.16.fin_a, f32[22,8,128]{2,1,0:T(8,128)} %get-tuple-element.17.half_a, f32[22,8,128]{2,1,0:T(8,128)} %get-tuple-element.18.fin_b, ...), custom_call_target="tpu_custom_call" | custom-call | tf_op jit(solution)/shard_map/pallas_call | solution.py:615

commit v3 on v2

--- a/solution.py
+++ b/solution.py
@@ -54,15 +54,15 @@
     grad_scale,
     tile_src, feat_t, send_rows, send_count, tiles_hbm, labels, w1s, w1n, w2s_t, w2n_t,
     fin_a, half_a, fin_b, half_b, fin_c, half_c,
-    tiles, xcat, slot_col, wide, w2p_t, order_v, order,
+    tiles, xcat, xsend, slot_col, wide, w2p_t, order_v, order,
     hot, hot_t, tiles_t, src, run, ptile,
     out1, recv1, xrecv, w1s_full, w1n_full, aggp, agg_recv, xfull, aggf,
     slope, hid, xa_t, pf, ycat, ypack, yown, yrecv, spack, srecv,
-    out2, recv2, stat, dlp, ret, recvb, gp, dlcat, dlcat_t, gcat,
+    out2, recv2, stat, hits, dlp, ret, recvb, gp, dlcat, dlcat_t, gcat,
     da, pa, db, pb, dc, pc, ra, rb, rc, ta, tb, tc, trecv,
     s_tiles, s_order, s_x, r_x, s_w, r_w, s_e1, r_e1, s_agg, r_agg, s_y, r_y, s_s, r_s, s_e2, r_e2,
     s_st, r_st, s_dl, r_dl, s_eb, r_eb, s_g, r_g, s_pair, r_pair, s_red, r_red,
-    s_t, r_t, s_fin, r_fin, s_half, r_half,
+    s_t, r_t, s_fin, r_fin, s_half, r_half, s_hit, r_hit,
 ):
     me = lax.axis_index("node")
     f = lax.axis_index("feat")
@@ -103,13 +103,18 @@
         pl.semaphore_signal(bar, inc=1, device_id=(lax.rem(me + i, NODES), f), device_id_type=MESH)
         return c
 
-    lax.fori_loop(1, NODES, hello, 0)
+    for lo, hi in ((25, 40), (1, 25), (40, NODES)):
+        lax.fori_loop(lo, hi, hello, 0)
     for i in range(1, FEATS):
         pl.semaphore_signal(bar, inc=1, device_id=(me, lax.rem(f + i, FEATS)), device_id_type=MESH)
 
     x0 = jnp.transpose(jnp.concatenate([feat_t[...].astype(F32), jnp.zeros((96, ROWS), F32)], axis=0))
     for q in range(4):
-        xcat[q] = lane_roll(x0, 32 * q).astype(BF)
+        shifted = lane_roll(x0, 32 * q)
+        xcat[q] = shifted.astype(BF)
+        part = shifted[128 * q:128 * q + 128]
+        xpack = part if q == 0 else xpack + part
+    xsend[...] = xpack.astype(BF)
 
     wide[0, 0:64, 0:64] = send_rows[...].astype(F32)
     turned = jnp.transpose(wide[0, 0:128, 0:128]).astype(I32)[0:64]
@@ -122,15 +127,22 @@
         return c
 
     lax.fori_loop(0, NODES, build_hot, 0, unroll=8)
+
+    def pack1(m, c):
+        d0 = pl.multiple_of(m * 32, 32)
+        acc = jnp.zeros((512, 128), F32)
+        for q in range(4):
+            acc = acc + dot(hot[pl.ds(d0, 32), 16 * q:16 * q + 16, :].reshape(512, ROWS), xcat[q])
+        out1[pl.ds(d0, 32)] = acc.astype(BF).reshape(32, 16, 128)
+        return c
+
+    lax.fori_loop(0, 2, pack1, 0)
+    recv1[me] = out1[me]
+    xrecv[f] = xsend[...]
     pl.semaphore_wait(bar, NODES - 1 + FEATS - 1)
 
     for j in range(RINGS):
         rr = ring_at(j)
-        d0 = pl.multiple_of(rr * 16, 16)
-        acc = jnp.zeros((256, 128), F32)
-        for q in range(4):
-            acc = acc + dot(hot[pl.ds(d0, 16), 16 * q:16 * q + 16, :].reshape(256, ROWS), xcat[q])
-        out1[pl.ds(d0, 16)] = acc.astype(BF).reshape(16, 16, 128)
 
         def send1(k, c):
             k = (16 if j < 3 else 15) - 1 - k + (0 if j < 3 else 1)
@@ -142,12 +154,10 @@
     for i in (2, 1, 3):
         g = lax.rem(f + i, FEATS)
         cols = pl.ds(pl.multiple_of(g * 256, 256), 256)
-        send(xcat.at[f], xrecv.at[f], s_x, r_x, me, g)
+        send(xsend, xrecv.at[f], s_x, r_x, me, g)
         send(w1s.at[:, cols], w1s_full.at[f], s_w.at[0], r_w.at[0], me, g)
         send(w1n.at[:, cols], w1n_full.at[f], s_w.at[1], r_w.at[1], me, g)
 
-    recv1[me] = out1[me]
-    xrecv[f] = xcat[f]
     own_cols = pl.ds(pl.multiple_of(f * 256, 256), 256)
     w1s_full[f] = w1s[:, own_cols]
     w1n_full[f] = w1n[:, own_cols]
@@ -192,6 +202,21 @@
     def row_bytes(buf, j):
         return buf.at[pl.ds(0, 15 if j == 3 else 16)]
 
+    group = lane128 // 32
+
+    def unpack_feats(ref, out):
+        for b in range(4):
+            acc = jnp.zeros((128, 128), F32)
+            for g in range(4):
+                acc = jnp.where(group == g, lane_roll(ref[g].astype(F32), 32 * (g - b)), acc)
+            out[128 * b:128 * b + 128, :] = acc.astype(BF)
+
+    wait_bytes(xrecv.at[three], r_x)
+    wait_bytes(w1s_full.at[three], r_w.at[0])
+    unpack_feats(xrecv, xfull)
+    slope[...] = dot(xfull[...], w1s_full[...].reshape(128, 256))
+    xa_t[0:128, :] = jnp.transpose(xfull[...])
+
     for j in (3, 1, 2, 0):
         rr = ring_at(j)
         wait_bytes(row_bytes(recv1, j), r_e1.at[rr])
@@ -212,26 +237,17 @@
         return dot(lhs, rhs)
 
     packed = jnp.zeros((128, 128), F32)
-    group = lane128 // 32
     for b in range(4):
         packed = packed + lane_roll(jnp.where(group == 0, tile_product(b), 0.0), 32 * b)
     aggp[...] = packed.astype(BF)
     to_feats(aggp, agg_recv, s_agg, r_agg, same=True)
     agg_recv[f] = aggp[...]
 
-    wait_bytes(xrecv.at[three], r_x)
-    wait_bytes(w1s_full.at[three], r_w.at[0])
     wait_bytes(w1n_full.at[three], r_w.at[1])
-    xfull[...] = xrecv[0] + xrecv[1] + xrecv[2] + xrecv[3]
-    pre0 = dot(xfull[...], w1s_full[...].reshape(128, 256))
     wait_bytes(agg_recv.at[three], r_agg)
-    for b in range(4):
-        acc = jnp.zeros((128, 128), F32)
-        for g in range(4):
-            acc = jnp.where(group == g, lane_roll(agg_recv[g].astype(F32), 32 * (g - b)), acc)
-        aggf[128 * b:128 * b + 128, :] = acc.astype(BF)
-
-    pre = pre0 + dot(aggf[...], w1n_full[...].reshape(128, 256))
+    unpack_feats(agg_recv, aggf)
+
+    pre = slope[...] + dot(aggf[...], w1n_full[...].reshape(128, 256))
     th = jnp.tanh(GELU_C * (pre + 0.044715 * (pre * pre * pre)))
     cdf = 0.5 * (1.0 + th)
     slope[...] = cdf + pre * (0.5 * (1.0 - th * th)) * (GELU_C * (1.0 + 3.0 * 0.044715 * (pre * pre)))
@@ -285,7 +301,6 @@
     recv2[me] = out2[me]
     for b in range(4):
         src[b] = ycat[0, 128 * b:128 * b + 128, :]
-    xa_t[0:128, :] = jnp.transpose(xfull[...])
     xa_t[128:256, :] = jnp.transpose(aggf[...])
 
     def turn_hot(y, c):
@@ -328,24 +343,24 @@
         want = mine & ((lab - CLS * f) == lane128)
         hit = jnp.sum(jnp.where(want, lg, 0.0), axis=1, keepdims=True)
         st = jnp.where(lane128 == 0, top, jnp.where(lane128 == 1, tot, jnp.where(lane128 == 2, hit, 0.0)))
-        stat[f, :, r] = jnp.transpose(st)[0:8, :]
+        st_t = jnp.transpose(st)
+        stat[f, b:b + 1, :] = st_t[0:1]
+        stat[f, 4 + b:5 + b, :] = st_t[1:2]
+        hits[f, b:b + 1, :] = st_t[2:3]
         pf[1, r, :] = ex
         pf[2, r, :] = jnp.where(want, 1.0, 0.0)
     to_feats(stat.at[f], stat, s_st, r_st, same=True)
     wait_bytes(stat.at[three], r_st)
 
-    tops = [stat[g, 0:1, :] for g in range(4)]
+    tops = [stat[g, 0:4, :] for g in range(4)]
     best = jnp.maximum(jnp.maximum(tops[0], tops[1]), jnp.maximum(tops[2], tops[3]))
     total = jnp.zeros_like(best)
-    hits = jnp.zeros_like(best)
     for g in range(4):
-        total = total + stat[g, 1:2, :] * jnp.exp(tops[g] - best)
-        hits = hits + stat[g, 2:3, :]
-    loss = jnp.sum(jnp.log(total) + best - hits)
-    factor = jnp.broadcast_to(jnp.exp(stat[f, 0:1, :] - best) / total, (128, ROWS))
+        total = total + stat[g, 4:8, :] * jnp.exp(tops[g] - best)
+    factor = jnp.exp(stat[f, 0:4, :] - best) / total
     for b in range(4):
         r = slice(128 * b, 128 * b + 128)
-        fac = jnp.transpose(factor[:, 128 * b:128 * b + 128])
+        fac = jnp.transpose(jnp.broadcast_to(factor[b:b + 1, :], (128, 128)))
         dl = ((pf[1, r, :] * fac - pf[2, r, :]) * grad_scale).astype(BF)
         rows = slice(128 * (b % 2), 128 * (b % 2) + 128)
         if b < 2:
@@ -355,6 +370,7 @@
         lhs = tiles_t[16 * b:16 * b + 16].reshape(2048, 128)
         ptile[16 * b:16 * b + 16] = dot(lhs, dl).reshape(16, 128, 128)
     to_feats(dlp.at[f], dlp, s_dl, r_dl, same=True)
+    to_feats(hits.at[f], hits, s_hit, r_hit, same=True)
 
     def gather_sum(t, acc):
         acc = acc * order[1, t].astype(F32) + ptile[order[0, t]]
@@ -447,6 +463,9 @@
 
         send(fin, half, s_half.at[k], r_half.at[k], partner, f)
 
+    wait_bytes(hits.at[three], r_hit)
+    hit_sum = hits[0, 0:4, :] + hits[1, 0:4, :] + hits[2, 0:4, :] + hits[3, 0:4, :]
+    loss = jnp.sum(jnp.log(total) + best - hit_sum)
     wait_bytes(dlp.at[three], r_dl)
     join(dlp, dlcat)
     dlcat_t[...] = jnp.transpose(dlcat[...])
@@ -472,14 +491,14 @@
     wait_bytes(gp.at[three], r_g)
     join(gp, gcat)
 
-    class_rows(dot(jnp.transpose(gcat[...]), hid[...]), db)
-    send(db.at[1 - core], pb, s_pair.at[1], r_pair.at[1], partner, f)
     bh = bh0 + dot(gcat[...], w2p_t[256:512, :])
     g1 = dot(xa_t[...], (bh * slope[...]).astype(BF))
     for l in range(2):
         for ch in range(CHIPS):
             dc[l, ch] = g1[g1_row(ch):g1_row(ch) + 8, 128 * l:128 * l + 128]
     send(dc.at[1 - core], pc, s_pair.at[2], r_pair.at[2], partner, f)
+    class_rows(dot(jnp.transpose(gcat[...]), hid[...]), db)
+    send(db.at[1 - core], pb, s_pair.at[1], r_pair.at[1], partner, f)
     wait_bytes(pc, r_pair.at[2])
     dc[core] = dc[core] + pc[...]
     for_chips(lambda p: send(dc.at[core, p], rc.at[chip], s_red.at[2], r_red.at[2], 2 * p + core, f))
@@ -529,6 +548,7 @@
     wait_bytes(recv2.at[n63], s_e2)
     wait_bytes(stat.at[three], s_st)
     wait_bytes(dlp.at[three], s_dl)
+    wait_bytes(hits.at[three], s_hit)
     wait_bytes(recvb.at[n63], s_eb)
     wait_bytes(gp.at[three], s_g)
     wait_bytes(pa, s_pair.at[0])
@@ -586,24 +606,24 @@
         in_specs=[pl.BlockSpec(memory_space=pltpu.SMEM)] + [whole] * 3 + [pl.BlockSpec(memory_space=pl.ANY)] + [whole] * 5,
         out_specs=(whole,) * 6,
         scratch_shapes=[
-            vm(64, 128, 128, dt=BF), vm(4, 512, 128, dt=BF), vm(64, 128, dt=I32), vm(2, 256, 256),
+            vm(64, 128, 128, dt=BF), vm(4, 512, 128, dt=BF), vm(128, 128, dt=BF), vm(64, 128, dt=I32), vm(2, 256, 256),
             vm(512, 256, dt=BF), vm(8, 128, dt=I32), pltpu.SMEM((8, 128), I32),
             vm(64, 64, 512, dt=BF), vm(4, 2, 512, 512, dt=BF), vm(64, 128, 128, dt=BF), vm(36, 128, 128, dt=BF),
             vm(64, 128, 128), vm(64, 128, 128),
-            vm(64, 16, 128, dt=BF), vm(64, 16, 128, dt=BF), vm(4, 512, 128, dt=BF),
+            vm(64, 16, 128, dt=BF), vm(64, 16, 128, dt=BF), vm(4, 128, 128, dt=BF),
             vm(4, 32, 256, dt=BF), vm(4, 32, 256, dt=BF), vm(128, 128, dt=BF), vm(4, 128, 128, dt=BF),
             vm(512, 128, dt=BF), vm(512, 128, dt=BF),
             vm(512, 256), vm(512, 256, dt=BF), vm(256, 512, dt=BF), vm(4, 512, 128),
             vm(2, 512, 128, dt=BF), vm(4, 256, 128, dt=BF), vm(4, 256, 128), vm(4, 256, 128, dt=BF),
             vm(4, 256, 128), vm(4, 256, 128),
-            vm(64, 32, 128, dt=BF), vm(64, 32, 128, dt=BF), vm(4, 8, 512), vm(4, 256, 128, dt=BF),
+            vm(64, 32, 128, dt=BF), vm(64, 32, 128, dt=BF), vm(4, 8, 128), vm(4, 8, 128), vm(4, 256, 128, dt=BF),
             vm(64, 32, 128, dt=BF), vm(64, 32, 128, dt=BF), vm(4, 256, 128, dt=BF),
             vm(512, 256, dt=BF), vm(256, 512, dt=BF), vm(512, 256, dt=BF),
             vm(2, TALL, 128), vm(TALL, 128), vm(2, TALL, 128), vm(TALL, 128), vm(2, 32, 8, 128), vm(32, 8, 128),
             vm(32, 8, 128), vm(32, 8, 128), vm(32, 8, 128), vm(8, 128), vm(8, 128), vm(8, 128), vm(4, 8, 128),
             dma, dma, dma, dma, dma((2,)), dma((2,)), dma, dma((4,)), dma, dma, dma, dma, dma, dma, dma, dma((4,)),
             dma, dma, dma, dma, dma, dma((4,)), dma, dma, dma((3,)), dma((3,)), dma((3,)), dma((3,)),
-            dma, dma, dma((3,)), dma((3,)), dma((3,)), dma((3,)),
+            dma, dma, dma((3,)), dma((3,)), dma((3,)), dma((3,)), dma, dma,
         ],
         compiler_params=pltpu.CompilerParams(
             collective_id=0, has_side_effects=True, vmem_limit_bytes=56 * 1024 * 1024

time: 104 us -> 102 us (0.981)
  Pallas kernels: 104 us -> 101 us
    pallas_call x1, Pallas kernels: 102 us -> 98.8 us  [shards(): pl.pallas_call(functools.partial(step_kernel, 1.0 / math.sqrt(ROWS * NODE...]
where the time goes in v3:
time: 102 us; the launch traced here: 101 us
  Pallas kernels  101 us (99%)
    pallas_call x1, Pallas kernels, shards(): pl.pallas_call(functools.partial(step_kernel, 1.0 / math.sqrt(ROWS * NODE...  98.8 us

profile of v3, /device:TPU:1, one launch (start us, length us, event | category | flops | bytes accessed | tf_op | source)
XLA Modules:
  0.0 101.5 jit_solution(2834359925220071612)
XLA Ops:
  0.6 98.8 %shard_map.137 = (f32[22,8,128]{2,1,0:T(8,128)}, f32[22,8,128]{2,1,0:T(8,128)}, f32[22,8,128]{2,1,0:T(8,128)}, f32[22,8,128]{2,1,0:T(8,128)}, f32[8,4,8,128]{3,2,1,0:T(8,128)}, /*index=5*/f32[8,4,8,128]{3,2,1,0:T(8,128)}) custom-call(s32[4,16]{1,0:T(4,128)} %tile_src.1, bf16[32,512]{1,0:T(8,128)(2,1)} %bitcast.12, s32[64,64]{1,0:T(8,128)} %bitcast.13, ...), custom_call_target="tpu_custom_call" | custom-call | tf_op jit(solution)/shard_map/pallas_call | solution.py:603
  99.5 2.0 %shard_map.138 = (f32[1,1]{1,0:T(1,128)}, f32[32,1024]{1,0:T(8,128)}, f32[32,1024]{1,0:T(8,128)}, f32[172,256]{1,0:T(8,128)}, f32[172,256]{1,0:T(8,128)}) custom-call(f32[22,8,128]{2,1,0:T(8,128)} %get-tuple-element.16.fin_a, f32[22,8,128]{2,1,0:T(8,128)} %get-tuple-element.17.half_a, f32[22,8,128]{2,1,0:T(8,128)} %get-tuple-element.18.fin_b, ...), custom_call_target="tpu_custom_call" | custom-call | tf_op jit(solution)/shard_map/pallas_call | solution.py:635

commit v4 on v3

--- a/solution.py
+++ b/solution.py
@@ -23,6 +23,8 @@
 CLS = 43
 TALL = 176
 CLS_TILES = TALL // 8
+MSG = 24
+RING_ROWS = 16 * MSG
 GELU_C = math.sqrt(2.0 / math.pi)
 
 
@@ -41,6 +43,19 @@
 
 def iota(shape, axis):
     return lax.broadcasted_iota(I32, shape, axis)
+
+
+def split_third(w):
+    n = w.shape[0]
+    at = iota((n, 16, 128), 2)
+    last = jnp.sum(jnp.where(at == iota((n, 16, 128), 1), w[:, 16:17, :], 0.0), axis=2, keepdims=True)
+    return jnp.where(at == CLS - 1, last, w[:, 0:16, :])
+
+
+def third_rest(col):
+    shape = col.shape
+    pick = (iota(shape, 2) == iota(shape, 1) + 2 * CLS) & (iota(shape, 1) < 16)
+    return jnp.sum(jnp.where(pick, col, 0.0), axis=1, keepdims=True)
 
 
 def g1_row(chip):
@@ -55,7 +70,7 @@
     tile_src, feat_t, send_rows, send_count, tiles_hbm, labels, w1s, w1n, w2s_t, w2n_t,
     fin_a, half_a, fin_b, half_b, fin_c, half_c,
     tiles, xcat, xsend, slot_col, wide, w2p_t, order_v, order,
-    hot, hot_t, tiles_t, src, run, ptile,
+    hot, hot3, hot_t, tiles_t, src, run, ptile,
     out1, recv1, xrecv, w1s_full, w1n_full, aggp, agg_recv, xfull, aggf,
     slope, hid, xa_t, pf, ycat, ypack, yown, yrecv, spack, srecv,
     out2, recv2, stat, hits, dlp, ret, recvb, gp, dlcat, dlcat_t, gcat,
@@ -190,6 +205,22 @@
     order_copy = pltpu.make_async_copy(order_v, order, s_order)
     order_copy.start()
 
+    def build_hot3(m, c):
+        cols = []
+        for d in (2 * m, 2 * m + 1):
+            cols.append(jnp.sum(jnp.where(lane(SLOTS) == d, slot_col[...], 0), axis=1, keepdims=True))
+        none = jnp.full((8, 1), -1, I32)
+        at = pl.ds(pl.multiple_of(m * 48, 48), 48)
+        for k, rows in enumerate((
+            [cols[0][0:24], cols[1][0:24]],
+            [cols[0][24:48], cols[1][24:48]],
+            [cols[0][48:64], none, cols[1][48:64], none],
+        )):
+            col = jnp.concatenate(rows, axis=0)
+            hot3[k, at, :] = jnp.where(col == lane(48, ROWS), 1.0, 0.0).astype(BF)
+        return c
+
+    lax.fori_loop(0, NODES // 2, build_hot3, 0, unroll=4)
     load_tiles.wait()
 
     def turn(t, c):
@@ -278,17 +309,22 @@
     for g in range(4):
         ys = ys + yrecv[g].astype(F32)
     yr = lane_roll(ys, 64)
-    ycat[0, 0:256, :] = jnp.where(low256, ys, 0.0).astype(BF)
-    ycat[0, 256:512, :] = jnp.where(low256, yr, 0.0).astype(BF)
-    ycat[1, 0:256, :] = jnp.where(low256, 0.0, yr).astype(BF)
-    ycat[1, 256:512, :] = jnp.where(low256, 0.0, ys).astype(BF)
+    y_lo = jnp.concatenate([jnp.where(low256, ys, 0.0), jnp.where(low256, yr, 0.0)], axis=0)
+    ycat[0] = y_lo.astype(BF)
+    ycat[1] = lane_roll(y_lo, CLS).astype(BF)
+    ycat[2] = lane_roll(jnp.where(lane(ROWS) < CLS - 1, y_lo, 0.0), 2 * CLS).astype(BF)
+    ycat[3] = jnp.broadcast_to(y_lo[:, CLS - 1:CLS], (ROWS, 128)).astype(BF)
 
     for j in range(RINGS):
         rr = ring_at(j)
         d0 = pl.multiple_of(rr * 16, 16)
-        acc = dot(hot[pl.ds(d0, 16), 0:32, :].reshape(512, ROWS), ycat[0])
-        acc = acc + dot(hot[pl.ds(d0, 16), 32:64, :].reshape(512, ROWS), ycat[1])
-        out2[pl.ds(d0, 16)] = acc.astype(BF).reshape(16, 32, 128)
+        at = pl.ds(pl.multiple_of(rr * RING_ROWS, RING_ROWS), RING_ROWS)
+        third = hot3[2, at, :]
+        acc = dot(hot3[0, at, :], ycat[0]) + dot(hot3[1, at, :], ycat[1]) + dot(third, ycat[2])
+        acc = acc.reshape(16, MSG, 128)
+        rest = third_rest(dot(third, ycat[3]).reshape(16, MSG, 128))
+        acc = jnp.where((iota((16, MSG, 128), 1) == 16) & (iota((16, MSG, 128), 2) >= 2 * CLS), rest, acc)
+        out2[pl.ds(d0, 16)] = acc.astype(BF)
 
         def send2(k, c):
             k = (16 if j < 3 else 15) - 1 - k + (0 if j < 3 else 1)
@@ -304,10 +340,9 @@
     xa_t[128:256, :] = jnp.transpose(aggf[...])
 
     def turn_hot(y, c):
-        d0 = pl.multiple_of(y * 16, 16)
-        for h in range(2):
+        for h in range(3):
             for k in range(4):
-                part = hot[pl.ds(d0, 16), 32 * h:32 * h + 32, 128 * k:128 * k + 128].reshape(512, 128)
+                part = hot3[h, pl.ds(pl.multiple_of(y * RING_ROWS, RING_ROWS), RING_ROWS), 128 * k:128 * k + 128]
                 hot_t[y, h, 128 * k:128 * k + 128, :] = jnp.transpose(part)
         return c
 
@@ -319,10 +354,9 @@
 
         def unpack2(k, c):
             b = rr * 8 + k
-            for p in range(2):
-                v = recv2[2 * b + p]
-                src[4 + b, 64 * p:64 * p + 32, :] = v
-                src[4 + b, 64 * p + 32:64 * p + 64, :] = lane_roll(v.astype(F32), 64).astype(BF)
+            v = recv2[pl.ds(2 * b, 2)].astype(F32)
+            both = jnp.concatenate([v, lane_roll(v, -CLS), split_third(lane_roll(v, -2 * CLS))], axis=1)
+            src[4 + b] = both.reshape(128, 128).astype(BF)
             return c
 
         lax.fori_loop(0, 8, unpack2, 0, unroll=4)
@@ -388,9 +422,13 @@
         def pack_back(k, c):
             to = rr * 8 + place_at(7 - k)
             blk = landed(4 + to)
-            for p in range(2):
-                v = blk[64 * p:64 * p + 32, :] + lane_roll(blk[64 * p + 32:64 * p + 64, :], 64)
-                ret[2 * to + p] = v.astype(BF)
+            blk = blk.reshape(2, 64, 128)
+            third = blk[:, 48:64, :]
+            rest = third_rest(jnp.broadcast_to(third[:, :, CLS - 1:CLS], (2, 16, 128)))
+            rest = jnp.where(iota((2, 8, 128), 1) == 0, rest, 0.0)
+            turned3 = lane_roll(jnp.where(iota((2, 16, 128), 2) < CLS - 1, third, 0.0), 2 * CLS)
+            v = blk[:, 0:24, :] + lane_roll(blk[:, 24:48, :], CLS) + jnp.concatenate([turned3, rest], axis=1)
+            ret[pl.ds(2 * to, 2)] = v.astype(BF)
             return c
 
         lax.fori_loop(0, 8, pack_back, 0, unroll=4)
@@ -477,13 +515,16 @@
     reduce_class(da, pa, ra, 0)
 
     g_sum = pf[3]
-    low = lane(ROWS) < 64
+    valid = lane(ROWS) < CLS
     for j in (3, 1, 2, 0):
         rr = ring_at(j)
         wait_bytes(row_bytes(recvb, j), r_eb.at[rr])
-        back = recvb[pl.ds(pl.multiple_of(rr * 16, 16), 16)].reshape(512, 128)
-        g_sum = g_sum + jnp.where(low, dot(hot_t[rr, 0], back), 0.0)
-        g_sum = g_sum + jnp.where(low, lane_roll(dot(hot_t[rr, 1], back), 64), 0.0)
+        back = recvb[pl.ds(pl.multiple_of(rr * 16, 16), 16)].astype(F32)
+        third = split_third(lane_roll(back, -2 * CLS))
+        third = jnp.concatenate([third, jnp.zeros((16, 8, 128), F32)], axis=1).reshape(RING_ROWS, 128).astype(BF)
+        back = back.reshape(RING_ROWS, 128).astype(BF)
+        g_sum = g_sum + jnp.where(valid, dot(hot_t[rr, 0], back) + dot(hot_t[rr, 2], third), 0.0)
+        g_sum = g_sum + jnp.where(valid, lane_roll(dot(hot_t[rr, 1], back), -CLS), 0.0)
     gp[f] = (g_sum[0:256] + lane_roll(g_sum[256:512], 64)).astype(BF)
     to_feats(gp.at[f], gp, s_g, r_g, same=True)
     spread_class(ra, ta, fin_a, 0)
@@ -608,16 +649,16 @@
         scratch_shapes=[
             vm(64, 128, 128, dt=BF), vm(4, 512, 128, dt=BF), vm(128, 128, dt=BF), vm(64, 128, dt=I32), vm(2, 256, 256),
             vm(512, 256, dt=BF), vm(8, 128, dt=I32), pltpu.SMEM((8, 128), I32),
-            vm(64, 64, 512, dt=BF), vm(4, 2, 512, 512, dt=BF), vm(64, 128, 128, dt=BF), vm(36, 128, 128, dt=BF),
+            vm(64, 64, 512, dt=BF), vm(3, 1536, 512, dt=BF), vm(4, 3, 512, 384, dt=BF), vm(64, 128, 128, dt=BF), vm(36, 128, 128, dt=BF),
             vm(64, 128, 128), vm(64, 128, 128),
             vm(64, 16, 128, dt=BF), vm(64, 16, 128, dt=BF), vm(4, 128, 128, dt=BF),
             vm(4, 32, 256, dt=BF), vm(4, 32, 256, dt=BF), vm(128, 128, dt=BF), vm(4, 128, 128, dt=BF),
             vm(512, 128, dt=BF), vm(512, 128, dt=BF),
             vm(512, 256), vm(512, 256, dt=BF), vm(256, 512, dt=BF), vm(4, 512, 128),
-            vm(2, 512, 128, dt=BF), vm(4, 256, 128, dt=BF), vm(4, 256, 128), vm(4, 256, 128, dt=BF),
+            vm(4, 512, 128, dt=BF), vm(4, 256, 128, dt=BF), vm(4, 256, 128), vm(4, 256, 128, dt=BF),
             vm(4, 256, 128), vm(4, 256, 128),
-            vm(64, 32, 128, dt=BF), vm(64, 32, 128, dt=BF), vm(4, 8, 128), vm(4, 8, 128), vm(4, 256, 128, dt=BF),
-            vm(64, 32, 128, dt=BF), vm(64, 32, 128, dt=BF), vm(4, 256, 128, dt=BF),
+            vm(64, MSG, 128, dt=BF), vm(64, MSG, 128, dt=BF), vm(4, 8, 128), vm(4, 8, 128), vm(4, 256, 128, dt=BF),
+            vm(64, MSG, 128, dt=BF), vm(64, MSG, 128, dt=BF), vm(4, 256, 128, dt=BF),
             vm(512, 256, dt=BF), vm(256, 512, dt=BF), vm(512, 256, dt=BF),
             vm(2, TALL, 128), vm(TALL, 128), vm(2, TALL, 128), vm(TALL, 128), vm(2, 32, 8, 128), vm(32, 8, 128),
             vm(32, 8, 128), vm(32, 8, 128), vm(32, 8, 128), vm(8, 128), vm(8, 128), vm(8, 128), vm(4, 8, 128),

time: 102 us -> 98.9 us (0.970)
  Pallas kernels: 101 us -> 98.2 us
    pallas_call x1, Pallas kernels: 98.8 us -> 96.2 us  [shards(): pl.pallas_call(functools.partial(step_kernel, 1.0 / math.sqrt(ROWS * NODE...]
where the time goes in v4:
time: 98.9 us; the launch traced here: 98.8 us
  Pallas kernels  98.2 us (99%)
    pallas_call x1, Pallas kernels, shards(): pl.pallas_call(functools.partial(step_kernel, 1.0 / math.sqrt(ROWS * NODE...  96.2 us
    pallas_call x1, Pallas kernels, shards(): pl.pallas_call(functools.partial(result_kernel, 1.0 / (ROWS * NODES)), ou...  2 us

profile of v4, /device:TPU:1, one launch (start us, length us, event | category | flops | bytes accessed | tf_op | source)
XLA Modules:
  0.0 98.8 jit_solution(15420775533579157368)
XLA Ops:
  0.6 96.2 %shard_map.137 = (f32[22,8,128]{2,1,0:T(8,128)}, f32[22,8,128]{2,1,0:T(8,128)}, f32[22,8,128]{2,1,0:T(8,128)}, f32[22,8,128]{2,1,0:T(8,128)}, f32[8,4,8,128]{3,2,1,0:T(8,128)}, /*index=5*/f32[8,4,8,128]{3,2,1,0:T(8,128)}) custom-call(s32[4,16]{1,0:T(4,128)} %tile_src.1, bf16[32,512]{1,0:T(8,128)(2,1)} %bitcast.12, s32[64,64]{1,0:T(8,128)} %bitcast.13, ...), custom_call_target="tpu_custom_call" | custom-call | tf_op jit(solution)/shard_map/pallas_call | solution.py:644
  96.8 2.0 %shard_map.138 = (f32[1,1]{1,0:T(1,128)}, f32[32,1024]{1,0:T(8,128)}, f32[32,1024]{1,0:T(8,128)}, f32[172,256]{1,0:T(8,128)}, f32[172,256]{1,0:T(8,128)}) custom-call(f32[22,8,128]{2,1,0:T(8,128)} %get-tuple-element.16.fin_a, f32[22,8,128]{2,1,0:T(8,128)} %get-tuple-element.17.half_a, f32[22,8,128]{2,1,0:T(8,128)} %get-tuple-element.18.fin_b, ...), custom_call_target="tpu_custom_call" | custom-call | tf_op jit(solution)/shard_map/pallas_call | solution.py:676

commit v5 on v4

--- a/solution.py
+++ b/solution.py
@@ -58,24 +58,17 @@
     return jnp.sum(jnp.where(pick, col, 0.0), axis=1, keepdims=True)
 
 
-def g1_row(chip):
-    y, z = chip // 8, chip % 8
-    keep = (y + z) % 4
-    rt = y * 2 + z // 4
-    return (rt // 4) * 128 + 32 * keep + 8 * (rt % 4)
-
-
 def step_kernel(
     grad_scale,
-    tile_src, feat_t, send_rows, send_count, tiles_hbm, labels, w1s, w1n, w2s_t, w2n_t,
+    tile_src_in, feat_in, rows_in, count_in, tiles_in, labels_in, w1s_in, w1n_in, w2s_in, w2n_in,
     fin_a, half_a, fin_b, half_b, fin_c, half_c,
-    tiles, xcat, xsend, slot_col, wide, w2p_t, order_v, order,
+    tile_src, feat_t, send_rows, send_count, labels, w1s, w1n, w2s_t, w2n_t, tiles, xcat, xsend, slot_col, wide, w2p_t, order_v, order,
     hot, hot3, hot_t, tiles_t, src, run, ptile,
     out1, recv1, xrecv, w1s_full, w1n_full, aggp, agg_recv, xfull, aggf,
     slope, hid, xa_t, pf, ycat, ypack, yown, yrecv, spack, srecv,
     out2, recv2, stat, hits, dlp, ret, recvb, gp, dlcat, dlcat_t, gcat,
     da, pa, db, pb, dc, pc, ra, rb, rc, ta, tb, tc, trecv,
-    s_tiles, s_order, s_x, r_x, s_w, r_w, s_e1, r_e1, s_agg, r_agg, s_y, r_y, s_s, r_s, s_e2, r_e2,
+    s_load, s_order, s_x, r_x, s_w, r_w, s_e1, r_e1, s_agg, r_agg, s_y, r_y, s_s, r_s, s_e2, r_e2,
     s_st, r_st, s_dl, r_dl, s_eb, r_eb, s_g, r_g, s_pair, r_pair, s_red, r_red,
     s_t, r_t, s_fin, r_fin, s_half, r_half, s_hit, r_hit,
 ):
@@ -109,8 +102,15 @@
     lane = lambda r, n=128: iota((r, n), 1)
     three = pl.ds(0, FEATS - 1)
 
-    load_tiles = pltpu.make_async_copy(tiles_hbm, tiles, s_tiles)
-    load_tiles.start()
+    loads = [
+        pltpu.make_async_copy(a, b, s_load.at[k])
+        for k, (a, b) in enumerate((
+            (rows_in, send_rows), (count_in, send_count), (feat_in, feat_t), (w1s_in, w1s), (w1n_in, w1n),
+            (tile_src_in, tile_src), (w2s_in, w2s_t), (w2n_in, w2n_t), (labels_in, labels), (tiles_in, tiles),
+        ))
+    ]
+    for load in loads:
+        load.start()
 
     bar = pltpu.get_barrier_semaphore()
 
@@ -122,6 +122,9 @@
         lax.fori_loop(lo, hi, hello, 0)
     for i in range(1, FEATS):
         pl.semaphore_signal(bar, inc=1, device_id=(me, lax.rem(f + i, FEATS)), device_id_type=MESH)
+
+    for load in loads[0:3]:
+        load.wait()
 
     x0 = jnp.transpose(jnp.concatenate([feat_t[...].astype(F32), jnp.zeros((96, ROWS), F32)], axis=0))
     for q in range(4):
@@ -154,6 +157,8 @@
     lax.fori_loop(0, 2, pack1, 0)
     recv1[me] = out1[me]
     xrecv[f] = xsend[...]
+    for load in loads[3:9]:
+        load.wait()
     pl.semaphore_wait(bar, NODES - 1 + FEATS - 1)
 
     for j in range(RINGS):
@@ -221,7 +226,7 @@
         return c
 
     lax.fori_loop(0, NODES // 2, build_hot3, 0, unroll=4)
-    load_tiles.wait()
+    loads[9].wait()
 
     def turn(t, c):
         tiles_t[t] = jnp.transpose(tiles[t])
@@ -535,47 +540,47 @@
     bh = bh0 + dot(gcat[...], w2p_t[256:512, :])
     g1 = dot(xa_t[...], (bh * slope[...]).astype(BF))
     for l in range(2):
-        for ch in range(CHIPS):
-            dc[l, ch] = g1[g1_row(ch):g1_row(ch) + 8, 128 * l:128 * l + 128]
+        dc[l] = g1[:, 128 * l:128 * l + 128]
     send(dc.at[1 - core], pc, s_pair.at[2], r_pair.at[2], partner, f)
     class_rows(dot(jnp.transpose(gcat[...]), hid[...]), db)
     send(db.at[1 - core], pb, s_pair.at[1], r_pair.at[1], partner, f)
     wait_bytes(pc, r_pair.at[2])
     dc[core] = dc[core] + pc[...]
-    for_chips(lambda p: send(dc.at[core, p], rc.at[chip], s_red.at[2], r_red.at[2], 2 * p + core, f))
-    rc[chip] = dc[core, chip]
+
+    def rows1(p):
+        m = p // 4
+        return pl.ds(pl.multiple_of((m // 4) * 128 + 32 * lax.rem(f + lax.rem(p, 4), 4) + 8 * lax.rem(m, 4), 8), 8)
+
+    for_chips(lambda p: send(dc.at[core, rows1(p)], rc.at[chip], s_red.at[2], r_red.at[2], 2 * p + core, f))
+    rc[chip] = dc[core, rows1(chip), :]
     reduce_class(db, pb, rb, 1)
 
     wait_bytes(rc.at[pl.ds(0, CHIPS - 1)], r_red.at[2])
     tc[...] = jnp.sum(rc[...], axis=0)
-    keep = lax.rem(ring + place, 4)
-    rt = ring * 2 + place // 4
-    kept = keep == f
-
-    @pl.when(jnp.logical_not(kept))
+    turn_by = lax.rem(chip, 4)
+    came_from = lax.rem(f - turn_by + 4, 4)
+
+    @pl.when(turn_by > 0)
     def _():
-        send(tc, trecv.at[f], s_t, r_t, me, keep)
+        send(tc, trecv, s_t, r_t, me, lax.rem(f + turn_by, 4))
 
     spread_class(rb, tb, fin_b, 1)
 
-    @pl.when(kept)
+    @pl.when(turn_by > 0)
     def _():
-        trecv[f] = tc[...]
-        wait_bytes(trecv.at[three], r_t)
-        for_chips(lambda p: send(trecv, fin_c.at[rt], s_fin.at[2], r_fin.at[2], 2 * p + core, f))
-        fin_c[rt] = trecv[...]
+        wait_bytes(trecv, r_t)
+
+    @pl.when(turn_by == 0)
+    def _():
+        trecv[...] = tc[...]
+
+    for_chips(lambda p: send(trecv, fin_c.at[chip // 4, came_from], s_fin.at[2], r_fin.at[2], 2 * p + core, f))
+    fin_c[chip // 4, came_from] = trecv[...]
 
     gather_class(fin_a, half_a, 0)
     gather_class(fin_b, half_b, 1)
 
-    @pl.when(kept)
-    def _():
-        wait_bytes(fin_c.at[pl.ds(0, 7)], r_fin.at[2])
-
-    @pl.when(jnp.logical_not(kept))
-    def _():
-        wait_bytes(fin_c, r_fin.at[2])
-
+    wait_bytes(rc.at[pl.ds(0, CHIPS - 1)], r_fin.at[2])
     send(fin_c, half_c, s_half.at[2], r_half.at[2], partner, f)
 
     n63, c31 = pl.ds(0, NODES - 1), pl.ds(0, CHIPS - 1)
@@ -606,13 +611,11 @@
         def _():
             wait_bytes(part.at[pl.ds(0, CLS_TILES)], s_red.at[k])
 
-    @pl.when(jnp.logical_not(kept))
+    wait_bytes(rc.at[c31], s_fin.at[2])
+
+    @pl.when(turn_by > 0)
     def _():
-        wait_bytes(trecv.at[0], s_t)
-
-    @pl.when(kept)
-    def _():
-        wait_bytes(ptile.at[c31, pl.ds(0, 32)], s_fin.at[2])
+        wait_bytes(trecv, s_t)
 
     for k, ref in enumerate((half_a, half_b, half_c)):
         wait_bytes(ref, s_half.at[k])
@@ -644,9 +647,11 @@
     parts = pl.pallas_call(
         functools.partial(step_kernel, 1.0 / math.sqrt(ROWS * NODES)),
         out_shape=(half_class,) * 4 + (half_first,) * 2,
-        in_specs=[pl.BlockSpec(memory_space=pltpu.SMEM)] + [whole] * 3 + [pl.BlockSpec(memory_space=pl.ANY)] + [whole] * 5,
+        in_specs=[pl.BlockSpec(memory_space=pltpu.HBM)] * 10,
         out_specs=(whole,) * 6,
         scratch_shapes=[
+            pltpu.SMEM((4, 16), I32), vm(32, 512, dt=BF), vm(64, 64, dt=I32), vm(1, 64, dt=I32), vm(4, 128, dt=I32),
+            vm(32, 1024, dt=BF), vm(32, 1024, dt=BF), vm(CLASSES, 256, dt=BF), vm(CLASSES, 256, dt=BF),
             vm(64, 128, 128, dt=BF), vm(4, 512, 128, dt=BF), vm(128, 128, dt=BF), vm(64, 128, dt=I32), vm(2, 256, 256),
             vm(512, 256, dt=BF), vm(8, 128, dt=I32), pltpu.SMEM((8, 128), I32),
             vm(64, 64, 512, dt=BF), vm(3, 1536, 512, dt=BF), vm(4, 3, 512, 384, dt=BF), vm(64, 128, 128, dt=BF), vm(36, 128, 128, dt=BF),
@@ -660,9 +665,9 @@
             vm(64, MSG, 128, dt=BF), vm(64, MSG, 128, dt=BF), vm(4, 8, 128), vm(4, 8, 128), vm(4, 256, 128, dt=BF),
             vm(64, MSG, 128, dt=BF), vm(64, MSG, 128, dt=BF), vm(4, 256, 128, dt=BF),
             vm(512, 256, dt=BF), vm(256, 512, dt=BF), vm(512, 256, dt=BF),
-            vm(2, TALL, 128), vm(TALL, 128), vm(2, TALL, 128), vm(TALL, 128), vm(2, 32, 8, 128), vm(32, 8, 128),
-            vm(32, 8, 128), vm(32, 8, 128), vm(32, 8, 128), vm(8, 128), vm(8, 128), vm(8, 128), vm(4, 8, 128),
-            dma, dma, dma, dma, dma((2,)), dma((2,)), dma, dma((4,)), dma, dma, dma, dma, dma, dma, dma, dma((4,)),
+            vm(2, TALL, 128), vm(TALL, 128), vm(2, TALL, 128), vm(TALL, 128), vm(2, 256, 128), vm(256, 128),
+            vm(32, 8, 128), vm(32, 8, 128), vm(32, 8, 128), vm(8, 128), vm(8, 128), vm(8, 128), vm(8, 128),
+            dma((10,)), dma, dma, dma, dma((2,)), dma((2,)), dma, dma((4,)), dma, dma, dma, dma, dma, dma, dma, dma((4,)),
             dma, dma, dma, dma, dma, dma((4,)), dma, dma, dma((3,)), dma((3,)), dma((3,)), dma((3,)),
             dma, dma, dma((3,)), dma((3,)), dma((3,)), dma((3,)), dma, dma,
         ],

time: 98.9 us -> 95.4 us (0.965)
  Pallas kernels: 98.2 us -> 94.6 us
    pallas_call x1, Pallas kernels: 96.2 us -> 92.6 us  [shards(): pl.pallas_call(functools.partial(step_kernel, 1.0 / math.sqrt(ROWS * NODE...]
where the time goes in v5:
time: 95.4 us; the launch traced here: 95.3 us
  Pallas kernels  94.6 us (99%)
    pallas_call x1, Pallas kernels, shards(): pl.pallas_call(functools.partial(step_kernel, 1.0 / math.sqrt(ROWS * NODE...  92.6 us
    pallas_call x1, Pallas kernels, shards(): pl.pallas_call(functools.partial(result_kernel, 1.0 / (ROWS * NODES)), ou...  2 us

profile of v5, /device:TPU:1, one launch (start us, length us, event | category | flops | bytes accessed | tf_op | source)
XLA Modules:
  0.0 95.3 jit_solution(3890786456118622784)
XLA Ops:
  0.6 92.6 %shard_map.137 = (f32[22,8,128]{2,1,0:T(8,128)}, f32[22,8,128]{2,1,0:T(8,128)}, f32[22,8,128]{2,1,0:T(8,128)}, f32[22,8,128]{2,1,0:T(8,128)}, f32[8,4,8,128]{3,2,1,0:T(8,128)}, /*index=5*/f32[8,4,8,128]{3,2,1,0:T(8,128)}) custom-call(s32[4,16]{1,0:T(4,128)} %tile_src_in.1, bf16[32,512]{1,0:T(8,128)(2,1)} %bitcast.12, s32[64,64]{1,0:T(8,128)} %bitcast.13, ...), custom_call_target="tpu_custom_call" | custom-call | tf_op jit(solution)/shard_map/pallas_call | solution.py:647
  93.3 2.0 %shard_map.138 = (f32[1,1]{1,0:T(1,128)}, f32[32,1024]{1,0:T(8,128)}, f32[32,1024]{1,0:T(8,128)}, f32[172,256]{1,0:T(8,128)}, f32[172,256]{1,0:T(8,128)}) custom-call(f32[22,8,128]{2,1,0:T(8,128)} %get-tuple-element.16.fin_a, f32[22,8,128]{2,1,0:T(8,128)} %get-tuple-element.17.half_a, f32[22,8,128]{2,1,0:T(8,128)} %get-tuple-element.18.fin_b, ...), custom_call_target="tpu_custom_call" | custom-call | tf_op jit(solution)/shard_map/pallas_call | solution.py:681

commit v6 on v5

--- a/solution.py
+++ b/solution.py
@@ -517,7 +517,6 @@
     for l in range(2):
         da[l, TALL - 8:TALL, :] = da[l, TALL - 8:TALL, :] + jnp.where(tail, loss, 0.0)
     send(da.at[1 - core], pa, s_pair.at[0], r_pair.at[0], partner, f)
-    reduce_class(da, pa, ra, 0)
 
     g_sum = pf[3]
     valid = lane(ROWS) < CLS
@@ -532,7 +531,7 @@
         g_sum = g_sum + jnp.where(valid, lane_roll(dot(hot_t[rr, 1], back), -CLS), 0.0)
     gp[f] = (g_sum[0:256] + lane_roll(g_sum[256:512], 64)).astype(BF)
     to_feats(gp.at[f], gp, s_g, r_g, same=True)
-    spread_class(ra, ta, fin_a, 0)
+    reduce_class(da, pa, ra, 0)
     bh0 = dot(dlcat[...], w2p_t[0:256, :])
     wait_bytes(gp.at[three], r_g)
     join(gp, gcat)
@@ -554,6 +553,7 @@
     for_chips(lambda p: send(dc.at[core, rows1(p)], rc.at[chip], s_red.at[2], r_red.at[2], 2 * p + core, f))
     rc[chip] = dc[core, rows1(chip), :]
     reduce_class(db, pb, rb, 1)
+    spread_class(ra, ta, fin_a, 0)
 
     wait_bytes(rc.at[pl.ds(0, CHIPS - 1)], r_red.at[2])
     tc[...] = jnp.sum(rc[...], axis=0)
@@ -672,12 +672,15 @@
             dma, dma, dma((3,)), dma((3,)), dma((3,)), dma((3,)), dma, dma,
         ],
         compiler_params=pltpu.CompilerParams(
-            collective_id=0, has_side_effects=True, vmem_limit_bytes=56 * 1024 * 1024
+            collective_id=0, has_side_effects=True, vmem_limit_bytes=44 * 1024 * 1024
         ),
-    )(
-        tile_src, features.T, send_rows[0], send_count, tile_val.reshape(TILES, 128, 128), labels.reshape(4, 128),
-        w_self1, w_neigh1, w_self2.T, w_neigh2.T,
-    )
+    )(*[
+        pltpu.with_memory_space_constraint(a, pltpu.HBM)
+        for a in (
+            tile_src, features.T, send_rows[0], send_count, tile_val.reshape(TILES, 128, 128), labels.reshape(4, 128),
+            w_self1, w_neigh1, w_self2.T, w_neigh2.T,
+        )
+    ])
     loss, gs1, gn1, gs2, gn2 = pl.pallas_call(
         functools.partial(result_kernel, 1.0 / (ROWS * NODES)),
         out_shape=(
@@ -689,6 +692,7 @@
         ),
         in_specs=[whole] * 6,
         out_specs=(whole,) * 5,
+        compiler_params=pltpu.CompilerParams(vmem_limit_bytes=8 * 1024 * 1024),
     )(*parts)
     return (loss[0, 0], gs1, gn1, gs2.T, gn2.T)
 

time: 95.4 us -> 93.5 us (0.980)
  Pallas kernels: 94.6 us -> 92.8 us
    pallas_call x1, Pallas kernels: 2 us -> 0.87 us  [shards(): pl.pallas_call(functools.partial(result_kernel, 1.0 / (ROWS * NODES)), ou...]
where the time goes in v6:
time: 93.5 us; the launch traced here: 93.4 us
  Pallas kernels  92.8 us (99%)
    pallas_call x1, Pallas kernels, shards(): pl.pallas_call(functools.partial(step_kernel, 1.0 / math.sqrt(ROWS * NODE...  91.9 us

profile of v6, /device:TPU:1, one launch (start us, length us, event | category | flops | bytes accessed | tf_op | source)
XLA Modules:
  0.0 93.4 jit_solution(6790499216697505639)
XLA Ops:
  0.6 91.9 %shard_map.137 = (f32[22,8,128]{2,1,0:T(8,128)S(1)}, f32[22,8,128]{2,1,0:T(8,128)S(1)}, f32[22,8,128]{2,1,0:T(8,128)S(1)}, f32[22,8,128]{2,1,0:T(8,128)S(1)}, f3...) custom-call(s32[4,16]{1,0:T(4,128)} %tile_src_in.1, bf16[32,512]{1,0:T(8,128)(2,1)} %bitcast.12, ...), custom_call_target="tpu_custom_call" | custom-call | tf_op jit(solution)/shard_map/pallas_call | solution.py:647
  92.6 0.9 shard_map.138

commit v7 on v6

--- a/solution.py
+++ b/solution.py
@@ -58,6 +58,19 @@
     return jnp.sum(jnp.where(pick, col, 0.0), axis=1, keepdims=True)
 
 
+def pack_slots(blk):
+    n = blk.shape[0]
+    third = blk[:, 48:64, :]
+    rest = third_rest(jnp.broadcast_to(third[:, :, CLS - 1:CLS], (n, 16, 128)))
+    rest = jnp.where(iota((n, 8, 128), 1) == 0, rest, 0.0)
+    turned = lane_roll(jnp.where(iota((n, 16, 128), 2) < CLS - 1, third, 0.0), 2 * CLS)
+    return blk[:, 0:24, :] + lane_roll(blk[:, 24:48, :], CLS) + jnp.concatenate([turned, rest], axis=1)
+
+
+def unpack_slots(v):
+    return jnp.concatenate([v, lane_roll(v, -CLS), split_third(lane_roll(v, -2 * CLS))], axis=1)
+
+
 def step_kernel(
     grad_scale,
     tile_src_in, feat_in, rows_in, count_in, tiles_in, labels_in, w1s_in, w1n_in, w2s_in, w2n_in,
@@ -70,7 +83,7 @@
     da, pa, db, pb, dc, pc, ra, rb, rc, ta, tb, tc, trecv,
     s_load, s_order, s_x, r_x, s_w, r_w, s_e1, r_e1, s_agg, r_agg, s_y, r_y, s_s, r_s, s_e2, r_e2,
     s_st, r_st, s_dl, r_dl, s_eb, r_eb, s_g, r_g, s_pair, r_pair, s_red, r_red,
-    s_t, r_t, s_fin, r_fin, s_half, r_half, s_hit, r_hit,
+    s_t, r_t, s_fin, r_fin, s_half, r_half, s_hit, r_hit, r_fin_c,
 ):
     me = lax.axis_index("node")
     f = lax.axis_index("feat")
@@ -298,7 +311,8 @@
     for half in range(2):
         v = dot_nt(hid[...], w2p_t[256 + 128 * half:256 + 128 * half + 128, :])
         for g in (2 * half, 2 * half + 1):
-            yv = pack_halves(v, g)
+            yv = jnp.where(lane(ROWS) < 64, v if g % 2 == 0 else lane_roll(v, 64), 0.0)
+            yv = pack_slots(yv.reshape(8, 64, 128)).reshape(192, 128)
             yown[g] = yv
             ypack[g] = yv.astype(BF)
     to_feats(ypack, yrecv, s_y, r_y)
@@ -307,14 +321,13 @@
         for g in (2 * half, 2 * half + 1):
             spack[g] = pack_halves(v, g)
     to_feats(spack, srecv, s_s, r_s)
-    yrecv[f] = jnp.zeros((256, 128), BF)
+    yrecv[f] = jnp.zeros((192, 128), BF)
     srecv[f] = spack[f]
     wait_bytes(yrecv.at[three], r_y)
     ys = yown[f]
     for g in range(4):
         ys = ys + yrecv[g].astype(F32)
-    yr = lane_roll(ys, 64)
-    y_lo = jnp.concatenate([jnp.where(low256, ys, 0.0), jnp.where(low256, yr, 0.0)], axis=0)
+    y_lo = jnp.where(lane(ROWS) < CLS, unpack_slots(ys.reshape(8, MSG, 128)).reshape(ROWS, 128), 0.0)
     ycat[0] = y_lo.astype(BF)
     ycat[1] = lane_roll(y_lo, CLS).astype(BF)
     ycat[2] = lane_roll(jnp.where(lane(ROWS) < CLS - 1, y_lo, 0.0), 2 * CLS).astype(BF)
@@ -360,8 +373,7 @@
         def unpack2(k, c):
             b = rr * 8 + k
             v = recv2[pl.ds(2 * b, 2)].astype(F32)
-            both = jnp.concatenate([v, lane_roll(v, -CLS), split_third(lane_roll(v, -2 * CLS))], axis=1)
-            src[4 + b] = both.reshape(128, 128).astype(BF)
+            src[4 + b] = unpack_slots(v).reshape(128, 128).astype(BF)
             return c
 
         lax.fori_loop(0, 8, unpack2, 0, unroll=4)
@@ -427,12 +439,7 @@
         def pack_back(k, c):
             to = rr * 8 + place_at(7 - k)
             blk = landed(4 + to)
-            blk = blk.reshape(2, 64, 128)
-            third = blk[:, 48:64, :]
-            rest = third_rest(jnp.broadcast_to(third[:, :, CLS - 1:CLS], (2, 16, 128)))
-            rest = jnp.where(iota((2, 8, 128), 1) == 0, rest, 0.0)
-            turned3 = lane_roll(jnp.where(iota((2, 16, 128), 2) < CLS - 1, third, 0.0), 2 * CLS)
-            v = blk[:, 0:24, :] + lane_roll(blk[:, 24:48, :], CLS) + jnp.concatenate([turned3, rest], axis=1)
+            v = pack_slots(blk.reshape(2, 64, 128))
             ret[pl.ds(2 * to, 2)] = v.astype(BF)
             return c
 
@@ -529,12 +536,17 @@
         back = back.reshape(RING_ROWS, 128).astype(BF)
         g_sum = g_sum + jnp.where(valid, dot(hot_t[rr, 0], back) + dot(hot_t[rr, 2], third), 0.0)
         g_sum = g_sum + jnp.where(valid, lane_roll(dot(hot_t[rr, 1], back), -CLS), 0.0)
-    gp[f] = (g_sum[0:256] + lane_roll(g_sum[256:512], 64)).astype(BF)
+    gp[f] = pack_slots(g_sum.reshape(8, 64, 128)).reshape(192, 128).astype(BF)
     to_feats(gp.at[f], gp, s_g, r_g, same=True)
     reduce_class(da, pa, ra, 0)
     bh0 = dot(dlcat[...], w2p_t[0:256, :])
     wait_bytes(gp.at[three], r_g)
-    join(gp, gcat)
+    for pair in range(2):
+        a, b = (
+            jnp.where(valid, unpack_slots(gp[g].astype(F32).reshape(8, MSG, 128)).reshape(ROWS, 128), 0.0)
+            for g in (2 * pair, 2 * pair + 1)
+        )
+        gcat[:, 128 * pair:128 * pair + 128] = (a + lane_roll(b, 64)).astype(BF)
 
     bh = bh0 + dot(gcat[...], w2p_t[256:512, :])
     g1 = dot(xa_t[...], (bh * slope[...]).astype(BF))
@@ -574,14 +586,17 @@
     def _():
         trecv[...] = tc[...]
 
-    for_chips(lambda p: send(trecv, fin_c.at[chip // 4, came_from], s_fin.at[2], r_fin.at[2], 2 * p + core, f))
+    for_chips(lambda p: send(trecv, fin_c.at[chip // 4, came_from], s_fin.at[2], r_fin_c.at[ring], 2 * p + core, f))
     fin_c[chip // 4, came_from] = trecv[...]
 
     gather_class(fin_a, half_a, 0)
     gather_class(fin_b, half_b, 1)
 
-    wait_bytes(rc.at[pl.ds(0, CHIPS - 1)], r_fin.at[2])
-    send(fin_c, half_c, s_half.at[2], r_half.at[2], partner, f)
+    for j in (3, 1, 2, 0):
+        rr = ring_at(j)
+        wait_bytes(rc.at[pl.ds(0, 7 if j == 3 else 8)], r_fin_c.at[rr])
+        part = pl.ds(2 * rr, 2)
+        send(fin_c.at[part], half_c.at[part], s_half.at[2], r_half.at[2], partner, f)
 
     n63, c31 = pl.ds(0, NODES - 1), pl.ds(0, CHIPS - 1)
     wait_bytes(recv1.at[n63], s_e1)
@@ -660,16 +675,16 @@
             vm(4, 32, 256, dt=BF), vm(4, 32, 256, dt=BF), vm(128, 128, dt=BF), vm(4, 128, 128, dt=BF),
             vm(512, 128, dt=BF), vm(512, 128, dt=BF),
             vm(512, 256), vm(512, 256, dt=BF), vm(256, 512, dt=BF), vm(4, 512, 128),
-            vm(4, 512, 128, dt=BF), vm(4, 256, 128, dt=BF), vm(4, 256, 128), vm(4, 256, 128, dt=BF),
+            vm(4, 512, 128, dt=BF), vm(4, 192, 128, dt=BF), vm(4, 192, 128), vm(4, 192, 128, dt=BF),
             vm(4, 256, 128), vm(4, 256, 128),
             vm(64, MSG, 128, dt=BF), vm(64, MSG, 128, dt=BF), vm(4, 8, 128), vm(4, 8, 128), vm(4, 256, 128, dt=BF),
-            vm(64, MSG, 128, dt=BF), vm(64, MSG, 128, dt=BF), vm(4, 256, 128, dt=BF),
+            vm(64, MSG, 128, dt=BF), vm(64, MSG, 128, dt=BF), vm(4, 192, 128, dt=BF),
             vm(512, 256, dt=BF), vm(256, 512, dt=BF), vm(512, 256, dt=BF),
             vm(2, TALL, 128), vm(TALL, 128), vm(2, TALL, 128), vm(TALL, 128), vm(2, 256, 128), vm(256, 128),
             vm(32, 8, 128), vm(32, 8, 128), vm(32, 8, 128), vm(8, 128), vm(8, 128), vm(8, 128), vm(8, 128),
             dma((10,)), dma, dma, dma, dma((2,)), dma((2,)), dma, dma((4,)), dma, dma, dma, dma, dma, dma, dma, dma((4,)),
             dma, dma, dma, dma, dma, dma((4,)), dma, dma, dma((3,)), dma((3,)), dma((3,)), dma((3,)),
-            dma, dma, dma((3,)), dma((3,)), dma((3,)), dma((3,)), dma, dma,
+            dma, dma, dma((3,)), dma((3,)), dma((3,)), dma((3,)), dma, dma, dma((4,)),
         ],
         compiler_params=pltpu.CompilerParams(
             collective_id=0, has_side_effects=True, vmem_limit_bytes=44 * 1024 * 1024

time: 93.5 us -> 93.4 us (level)
  no operation moved by 1% of the time
where the time goes in v7:
time: 93.4 us; the launch traced here: 93.3 us
  Pallas kernels  92.7 us (99%)
    pallas_call x1, Pallas kernels, shards(): pl.pallas_call(functools.partial(step_kernel, 1.0 / math.sqrt(ROWS * NODE...  91.8 us

profile of v7, /device:TPU:1, one launch (start us, length us, event | category | flops | bytes accessed | tf_op | source)
XLA Modules:
  0.0 93.3 jit_solution(12979123358468852098)
XLA Ops:
  0.6 91.8 %shard_map.137 = (f32[22,8,128]{2,1,0:T(8,128)S(1)}, f32[22,8,128]{2,1,0:T(8,128)S(1)}, f32[22,8,128]{2,1,0:T(8,128)S(1)}, f32[22,8,128]{2,1,0:T(8,128)S(1)}, f3...) custom-call(s32[4,16]{1,0:T(4,128)} %tile_src_in.1, bf16[32,512]{1,0:T(8,128)(2,1)} %bitcast.12, ...), custom_call_target="tpu_custom_call" | custom-call | tf_op jit(solution)/shard_map/pallas_call | solution.py:662
  92.5 0.9 shard_map.138

commit v8 on v7

--- a/solution.py
+++ b/solution.py
@@ -278,7 +278,7 @@
                     src[4 + b, 64 * p + 16 * q:64 * p + 16 * q + 16, :] = lane_roll(v, -32 * q).astype(BF)
             return c
 
-        lax.fori_loop(0, 8, unpack1, 0, unroll=4)
+        lax.fori_loop(0, 8, unpack1, 0, unroll=8)
 
     def tile_product(b):
         lhs = jnp.concatenate([tiles[16 * b + k] for k in range(16)], axis=1)
@@ -376,7 +376,7 @@
             src[4 + b] = unpack_slots(v).reshape(128, 128).astype(BF)
             return c
 
-        lax.fori_loop(0, 8, unpack2, 0, unroll=4)
+        lax.fori_loop(0, 8, unpack2, 0, unroll=8)
 
     wait_bytes(srecv.at[three], r_s)
     ss = srecv[0] + srecv[1] + srecv[2] + srecv[3]
@@ -428,7 +428,7 @@
         run[t] = acc
         return acc
 
-    lax.fori_loop(0, TILES, gather_sum, jnp.zeros((128, 128), F32), unroll=4)
+    lax.fori_loop(0, TILES, gather_sum, jnp.zeros((128, 128), F32), unroll=8)
 
     def landed(j):
         return run[order[2, j]] * order[3, j].astype(F32)
@@ -443,7 +443,7 @@
             ret[pl.ds(2 * to, 2)] = v.astype(BF)
             return c
 
-        lax.fori_loop(0, 8, pack_back, 0, unroll=4)
+        lax.fori_loop(0, 8, pack_back, 0, unroll=8)
 
         def send_back(k, c):
             k = (16 if j < 3 else 15) - 1 - k + (0 if j < 3 else 1)

time: 93.4 us -> 93.2 us (level)
  no operation moved by 1% of the time
where the time goes in v8:
time: 93.2 us; the launch traced here: 93.1 us
  Pallas kernels  92.5 us (99%)
    pallas_call x1, Pallas kernels, shards(): pl.pallas_call(functools.partial(step_kernel, 1.0 / math.sqrt(ROWS * NODE...  91.6 us

profile of v8, /device:TPU:1, one launch (start us, length us, event | category | flops | bytes accessed | tf_op | source)
XLA Modules:
  0.0 93.1 jit_solution(9144135245006701946)
XLA Ops:
  0.6 91.6 %shard_map.137 = (f32[22,8,128]{2,1,0:T(8,128)S(1)}, f32[22,8,128]{2,1,0:T(8,128)S(1)}, f32[22,8,128]{2,1,0:T(8,128)S(1)}, f32[22,8,128]{2,1,0:T(8,128)S(1)}, f3...) custom-call(s32[4,16]{1,0:T(4,128)} %tile_src_in.1, bf16[32,512]{1,0:T(8,128)(2,1)} %bitcast.12, ...), custom_call_target="tpu_custom_call" | custom-call | tf_op jit(solution)/shard_map/pallas_call | solution.py:662
  92.3 0.9 shard_map.138
